TPU v7x, 256 devices: a whole 4x4x8 slice. The times are simulated.
256 devices in a mesh: rows: 32 (over y, z), samples: 8 (over x, core).
Axes of the slice: x: 4, y: 4, z: 8, core: 2. Of those that a mesh axis runs over, the one named last changes fastest.
Arguments:
- matrix_block: bfloat16 [32768, 20480], P('rows', 'samples'), may hold values from -6 to 6
- sketch_matrix: bfloat16 [20480, 384], P('samples'), may hold values from -0.0390625 to 0.0390625
- local_pivots: int32 [32, 3, 256], P('rows'), may hold values from 0 to 511, as said below
- upper_pivots: int32 [30, 256], replicated, may hold values from 0 to 511, as said below
Outputs:
- leaf_basis: float32 [32768, 384], P(('rows', 'samples'))
- device_basis: float32 [16384, 384], P('rows')
- inner_basis: float32 [16384, 384], P('rows')
Inputs may be any that keep to these rules, and one draw needn't show every extreme that they name: `local_pivots`: each row holds 256 distinct indices. `upper_pivots`: each row holds 256 distinct indices.
All inputs are finite; a program needn't handle non-finite values.
Results may differ from a plain program's by a relative error of at most 0.0003.
Values sent between devices are 32-bit elements; how exact they have to be, the bound alone decides.
A program may use at most 128 MiB of HBM per device.

v0:
```python
import math

import jax
import jax.numpy as jnp
from jax import lax
from jax.sharding import PartitionSpec as P


def partner_2(block, axis, bit):
    count = lax.axis_size(axis)
    route = []
    for low in range(count):
        high = low | 1 << bit
        if high != low and high < count:
            route += [(low, high), (high, low)]
    return lax.ppermute(block, axis, route)


def matmul_high(left, right):
    return jnp.dot(left, right, precision=lax.Precision.HIGHEST, preferred_element_type=jnp.float32)


def inverse_factor(gram_matrix):
    order = gram_matrix.shape[0]
    if order <= 48:
        lower_factor = jnp.linalg.cholesky(gram_matrix)
        identity = jnp.eye(order, dtype=jnp.float32)
        return jax.scipy.linalg.solve_triangular(lower_factor, identity, lower=True)
    half = order // 2
    top_inverse = inverse_factor(gram_matrix[:half, :half])
    below = matmul_high(gram_matrix[half:, :half], top_inverse.T)
    schur = gram_matrix[half:, half:] - matmul_high(below, below.T)
    bottom_inverse = inverse_factor(schur)
    corner = -matmul_high(matmul_high(bottom_inverse, below), top_inverse)
    upper_rows = jnp.concatenate([top_inverse, jnp.zeros((half, order - half), jnp.float32)], 1)
    lower_rows = jnp.concatenate([corner, bottom_inverse], 1)
    return jnp.concatenate([upper_rows, lower_rows], 0)


def basis_of(stacked):
    gram_matrix = matmul_high(stacked.T, stacked)
    inverse = inverse_factor(gram_matrix)
    return matmul_high(stacked, inverse.T) * math.sqrt(stacked.shape[0])


def select_rows(matrix_rows, indices):
    return jnp.take(matrix_rows, indices, axis=0)


def keep_if_owner(chosen, new_basis, position, height, tree_depth):
    low_bits = position & (1 << height) - 1
    is_owner = low_bits == 1 << height - 1
    if height == tree_depth:
        is_owner = jnp.logical_or(is_owner, position == 0)
    return jnp.where(is_owner, new_basis, chosen)


def climb_tree(current, first_height, last_height, tree_depth, position, upper_pivots, chosen):
    for height in range(first_height, last_height + 1):
        partner = partner_2(current, "rows", height - 1)
        on_right = position >> height - 1 & 1 == 1
        left_part = jnp.where(on_right, partner, current)
        right_part = jnp.where(on_right, current, partner)
        stacked = jnp.concatenate([left_part, right_part], 0)
        chosen = keep_if_owner(chosen, basis_of(stacked), position, height, tree_depth)
        if height < tree_depth:
            node_row = (1 << tree_depth - height) + (position >> height) - 2
            indices = lax.dynamic_index_in_dim(upper_pivots, node_row, 0, keepdims=False)
            current = select_rows(stacked, indices)
    return (current, chosen)


def on_device(matrix_block, sketch_matrix, local_pivots, upper_pivots):
    leaf_rows = matrix_block.shape[0] // 2
    partial_value = jnp.dot(matrix_block, sketch_matrix, preferred_element_type=jnp.float32)
    pivots = local_pivots[0]
    summed = lax.psum(partial_value, "samples")
    first_leaf = summed[:leaf_rows]
    second_leaf = summed[leaf_rows:]
    leaf_bases = jnp.concatenate([basis_of(first_leaf), basis_of(second_leaf)], 0)
    share_rows = leaf_bases.shape[0] // lax.axis_size("samples")
    leaf_out = lax.dynamic_slice_in_dim(
        leaf_bases, lax.axis_index("samples") * share_rows, share_rows, 0
    )
    skeleton_a = select_rows(first_leaf, pivots[0])
    skeleton_b = select_rows(second_leaf, pivots[1])
    stacked = jnp.concatenate([skeleton_a, skeleton_b], 0)
    device_out = basis_of(stacked)
    current = select_rows(stacked, pivots[2])
    tree_depth = lax.axis_size("rows").bit_length() - 1
    position = lax.axis_index("rows")
    chosen = jnp.zeros_like(device_out)
    current, chosen = climb_tree(current, 1, tree_depth, tree_depth, position, upper_pivots, chosen)
    return (leaf_out, device_out, chosen)


def solution(mesh):
    in_specs = (P("rows", "samples"), P("samples", None), P("rows", None, None), P())
    out_specs = (P(("rows", "samples"), None), P("rows", None), P("rows", None))
    return jax.shard_map(
        on_device, mesh=mesh, in_specs=in_specs, out_specs=out_specs, check_vma=False
    )
```

profile of v0, /device:TPU:1, one launch (start us, length us, event | category | flops | bytes accessed | tf_op | source)
XLA Modules:
  0.0 929.4 jit_solution(7931484030356408931)
XLA Ops:
  8.7 6.5 fusion.797
  20.2 66.2 %all-reduce.58.cloned.1.call-done = f32[1024,384]{1,0:T(8,128)} async-done(((f32[1024,384]{1,0:T(8,128)}), f32[1024,384]{1,0:T(8,128)}) %all-reduce.58.cloned.1.call-update) | async-done | bytes 1572880 | tf_op jit(solution)/shard_map/psum | solution.py:77
  89.6 4.4 cholesky.1062
  99.7 4.4 cholesky.1073
  110.4 4.4 cholesky.1084
  120.6 4.4 cholesky.1095
  132.0 4.4 cholesky.1106
  142.2 4.4 cholesky.1117
  153.3 4.4 cholesky.1128
  167.7 4.4 cholesky.974
  177.8 4.4 cholesky.985
  188.5 4.4 cholesky.996
  198.8 4.4 cholesky.1007
  210.2 4.4 cholesky.1018
  220.4 4.4 cholesky.1029
  231.3 4.4 cholesky.1040
  251.8 4.4 cholesky.1150
  261.9 4.4 cholesky.1161
  274.6 5.1 cholesky.1172
  304.9 4.6 cholesky.1194
  315.3 4.4 cholesky.1205
  326.0 4.4 cholesky.1216
  343.9 5.7 cholesky.1139
  353.1 5.0 custom-call.83
  368.5 5.1 cholesky.1051
  375.5 5.0 custom-call.75
  389.7 4.4 cholesky.1227
  418.0 4.4 cholesky.1590
  428.1 4.4 cholesky.1601
  438.8 4.4 cholesky.1612
  449.1 4.5 cholesky.1623
  460.6 4.4 cholesky.1634
  470.8 4.4 cholesky.1645
  481.6 4.4 cholesky.1656
  491.9 4.4 cholesky.1667
  509.6 14.6 %collective-permute-done.1 = f32[256,384]{1,0:T(8,128)S(1)} collective-permute-done((f32[256,384]{1,0:T(8,128)S(1)}, f32[256,384]{1,0:T(8,128)S(1)}, u32[]{:S(2)}, u32[]{:S(2)}) %collective-permute-start.1) | collective-permute-done | bytes 393248 | tf_op jit(solution)/shard_map/ppermute | solution.py:16
  526.0 4.4 cholesky.1502
  536.2 4.4 cholesky.1513
  547.1 4.4 cholesky.1524
  557.5 4.4 cholesky.1535
  569.0 4.4 cholesky.1546
  579.4 4.5 cholesky.1557
  590.4 4.4 cholesky.1568
  600.8 4.4 cholesky.1579
  619.7 15.5 %collective-permute-done.2 = f32[256,384]{1,0:T(8,128)S(1)} collective-permute-done((f32[256,384]{1,0:T(8,128)S(1)}, f32[256,384]{1,0:T(8,128)S(1)}, u32[]{:S(2)}, u32[]{:S(2)}) %collective-permute-start.2) | collective-permute-done | bytes 393248 | tf_op jit(solution)/shard_map/ppermute | solution.py:16
  637.1 4.4 cholesky.1414
  647.3 4.4 cholesky.1425
  658.1 4.4 cholesky.1436
  668.6 4.4 cholesky.1447
  680.1 4.4 cholesky.1458
  690.4 4.8 cholesky.1469
  701.6 4.4 cholesky.1480
  712.1 4.4 cholesky.1491
  728.4 4.8 collective-permute-done.3
  735.1 4.4 cholesky.1326
  745.3 4.4 cholesky.1337
  756.2 4.4 cholesky.1348
  766.6 4.4 cholesky.1359
  778.1 4.4 cholesky.1370
  788.5 4.5 cholesky.1381
  799.4 4.4 cholesky.1392
  833.5 4.4 cholesky.1238
  876.5 4.4 cholesky.1282
  886.8 4.6 cholesky.1293
  (1017 shorter events, 538.1 us)
Async XLA Ops:
  7.2 1.6 copy-start
  7.2 79.1 %all-reduce.58.cloned.1.call-start = ((), (), s32[]{:S(2)}) async-start(), calls=%async_computation | async-start | bytes 3145728 | tf_op jit(solution)/shard_map/psum | solution.py:77
  109.7 55.4 %copy-start.12 = (f32[96,96]{1,0:T(8,128)}, f32[96,96]{1,0:T(8,128)S(1)}, u32[]{:S(2)}) copy-start(f32[96,96]{1,0:T(8,128)S(1)} %select_maximum_fusion.37) | copy-start | bytes 110596
  120.3 44.8 %copy-start.46 = (f32[48,96]{1,0:T(8,128)}, f32[48,96]{1,0:T(8,128)S(1)}, u32[]{:S(2)}) copy-start(f32[48,96]{1,0:T(8,128)S(1)} %concatenate.550) | copy-start | bytes 55300
  130.2 34.8 %copy-start.34 = (f32[48,48]{1,0:T(8,128)}, f32[48,48]{1,0:T(8,128)S(1)}, u32[]{:S(2)}) copy-start(f32[48,48]{1,0:T(8,128)S(1)} %fusion.110) | copy-start | bytes 27652
  130.6 34.5 %copy-start.50 = (f32[48,48]{1,0:T(8,128)}, f32[48,48]{1,0:T(8,128)S(1)}, u32[]{:S(2)}) copy-start(f32[48,48]{1,0:T(8,128)S(1)} %convolution_negate_fusion.50) | copy-start | bytes 27652
  131.0 34.1 %copy-start.61 = (f32[96,96]{1,0:T(8,128)}, f32[96,96]{1,0:T(8,128)S(1)}, u32[]{:S(2)}) copy-start(f32[96,96]{1,0:T(8,128)S(1)} %convolution_negate_fusion.21) | copy-start | bytes 110596
  131.5 34.4 %copy-start.2 = (f32[1024,384]{1,0:T(8,128)S(1)}, f32[1024,384]{1,0:T(8,128)}, u32[]{:S(2)}) copy-start(f32[1024,384]{1,0:T(8,128)} %all-reduce.58.cloned.1.call-done) | copy-start | bytes 4718596
  152.6 12.5 %copy-start.8 = (f32[96,96]{1,0:T(8,128)}, f32[96,96]{1,0:T(8,128)S(1)}, u32[]{:S(2)}) copy-start(f32[96,96]{1,0:T(8,128)S(1)} %select_maximum_fusion.36) | copy-start | bytes 110596
  152.9 12.2 %copy-start.4 = (f32[96,96]{1,0:T(8,128)}, f32[96,96]{1,0:T(8,128)S(1)}, u32[]{:S(2)}) copy-start(f32[96,96]{1,0:T(8,128)S(1)} %fusion.367) | copy-start | bytes 110596
  153.2 12.0 %copy-start.17 = (f32[96,96]{0,1:T(8,128)}, f32[96,96]{0,1:T(8,128)S(1)}, u32[]{:S(2)}) copy-start(f32[96,96]{0,1:T(8,128)S(1)} %convolution_subtract_fusion.20) | copy-start | bytes 110596
  162.9 24.8 %copy-start.29 = (f32[48,48]{1,0:T(8,128)}, f32[48,48]{1,0:T(8,128)S(1)}, u32[]{:S(2)}) copy-start(f32[48,48]{1,0:T(8,128)S(1)} %fusion.104) | copy-start | bytes 27652
  187.8 55.3 %copy-start.13 = (f32[96,96]{1,0:T(8,128)}, f32[96,96]{1,0:T(8,128)S(1)}, u32[]{:S(2)}) copy-start(f32[96,96]{1,0:T(8,128)S(1)} %select_maximum_fusion.39) | copy-start | bytes 110596
  198.1 45.0 %copy-start.47 = (f32[48,96]{1,0:T(8,128)}, f32[48,96]{1,0:T(8,128)S(1)}, u32[]{:S(2)}) copy-start(f32[48,96]{1,0:T(8,128)S(1)} %concatenate.529) | copy-start | bytes 55300
  208.5 34.7 %copy-start.35 = (f32[48,48]{1,0:T(8,128)}, f32[48,48]{1,0:T(8,128)S(1)}, u32[]{:S(2)}) copy-start(f32[48,48]{1,0:T(8,128)S(1)} %fusion.126) | copy-start | bytes 27652
  208.8 34.3 %copy-start.51 = (f32[48,48]{1,0:T(8,128)}, f32[48,48]{1,0:T(8,128)S(1)}, u32[]{:S(2)}) copy-start(f32[48,48]{1,0:T(8,128)S(1)} %convolution_negate_fusion.54) | copy-start | bytes 27652
  209.2 33.9 %copy-start.62 = (f32[96,96]{1,0:T(8,128)}, f32[96,96]{1,0:T(8,128)S(1)}, u32[]{:S(2)}) copy-start(f32[96,96]{1,0:T(8,128)S(1)} %convolution_negate_fusion.23) | copy-start | bytes 110596
  230.6 12.5 %copy-start.9 = (f32[96,96]{1,0:T(8,128)}, f32[96,96]{1,0:T(8,128)S(1)}, u32[]{:S(2)}) copy-start(f32[96,96]{1,0:T(8,128)S(1)} %select_maximum_fusion.38) | copy-start | bytes 110596
  231.0 12.2 %copy-start.5 = (f32[96,96]{1,0:T(8,128)}, f32[96,96]{1,0:T(8,128)S(1)}, u32[]{:S(2)}) copy-start(f32[96,96]{1,0:T(8,128)S(1)} %fusion.371) | copy-start | bytes 110596
  231.2 12.0 %copy-start.18 = (f32[96,96]{0,1:T(8,128)}, f32[96,96]{0,1:T(8,128)S(1)}, u32[]{:S(2)}) copy-start(f32[96,96]{0,1:T(8,128)S(1)} %convolution_subtract_fusion.22) | copy-start | bytes 110596
  241.0 2.2 copy-start.30
  271.9 29.3 %copy-start.14 = (f32[96,96]{1,0:T(8,128)}, f32[96,96]{1,0:T(8,128)S(1)}, u32[]{:S(2)}) copy-start(f32[96,96]{1,0:T(8,128)S(1)} %select_maximum_fusion.35) | copy-start | bytes 110596
  299.9 1.5 copy-start.36
  303.3 34.6 %copy-start.3 = (f32[192,192]{1,0:T(8,128)}, f32[192,192]{1,0:T(8,128)S(1)}, u32[]{:S(2)}) copy-start(f32[192,192]{1,0:T(8,128)S(1)} %fusion.257) | copy-start | bytes 442372
  303.3 34.6 %copy-start.15 = (f32[96,96]{1,0:T(8,128)S(1)}, f32[96,96]{1,0:T(8,128)}, u32[]{:S(2)}) copy-start(f32[96,96]{1,0:T(8,128)} %copy-done.14) | copy-start | bytes 110596
  303.3 34.6 %copy-start.37 = (f32[48,48]{1,0:T(8,128)S(1)}, f32[48,48]{1,0:T(8,128)}, u32[]{:S(2)}) copy-start(f32[48,48]{1,0:T(8,128)} %copy-done.36) | copy-start | bytes 27652
  303.3 34.6 %copy-start.48 = (f32[48,96]{1,0:T(8,128)S(1)}, f32[48,96]{1,0:T(8,128)}, u32[]{:S(2)}) copy-start(f32[48,96]{1,0:T(8,128)} %concatenate.573) | copy-start | bytes 55300
  303.3 34.6 %copy-start.53 = (f32[48,48]{1,0:T(8,128)S(1)}, f32[48,48]{1,0:T(8,128)}, u32[]{:S(2)}) copy-start(f32[48,48]{1,0:T(8,128)} %copy-done.52) | copy-start | bytes 27652
  325.4 12.5 %copy-start.10 = (f32[96,96]{1,0:T(8,128)}, f32[96,96]{1,0:T(8,128)S(1)}, u32[]{:S(2)}) copy-start(f32[96,96]{1,0:T(8,128)S(1)} %select_maximum_fusion.34) | copy-start | bytes 110596
  325.7 12.2 %copy-start.6 = (f32[96,96]{1,0:T(8,128)}, f32[96,96]{1,0:T(8,128)S(1)}, u32[]{:S(2)}) copy-start(f32[96,96]{1,0:T(8,128)S(1)} %fusion.363) | copy-start | bytes 110596
  325.9 11.9 %copy-start.20 = (f32[96,96]{0,1:T(8,128)}, f32[96,96]{0,1:T(8,128)S(1)}, u32[]{:S(2)}) copy-start(f32[96,96]{0,1:T(8,128)S(1)} %convolution_subtract_fusion.18) | copy-start | bytes 110596
  335.7 2.2 copy-start.32
  358.1 8.2 copy-start.19
  358.1 8.2 copy-start.31
  359.1 5.2 copy-start.22
  360.9 5.4 copy-start.41
  363.0 3.3 copy-start.57
  364.3 24.3 %copy-start.21 = (f32[96,96]{0,1:T(8,128)S(1)}, f32[96,96]{0,1:T(8,128)}, u32[]{:S(2)}) copy-start(f32[96,96]{0,1:T(8,128)} %copy-done.20) | copy-start | bytes 110596
  364.3 36.1 %copy-start.33 = (f32[48,48]{1,0:T(8,128)S(1)}, f32[48,48]{1,0:T(8,128)}, u32[]{:S(2)}) copy-start(f32[48,48]{1,0:T(8,128)} %copy-done.32) | copy-start | bytes 27652
  364.3 36.2 %copy-start.7 = (f32[96,96]{1,0:T(8,128)S(1)}, f32[96,96]{1,0:T(8,128)}, u32[]{:S(2)}) copy-start(f32[96,96]{1,0:T(8,128)} %copy-done.6) | copy-start | bytes 110596
  364.3 37.2 %copy-start.11 = (f32[96,96]{1,0:T(8,128)S(1)}, f32[96,96]{1,0:T(8,128)}, u32[]{:S(2)}) copy-start(f32[96,96]{1,0:T(8,128)} %copy-done.10) | copy-start | bytes 110596
  381.5 20.0 %copy-start.23 = (f32[48,48]{1,0:T(8,128)}, f32[48,48]{1,0:T(8,128)S(1)}, u32[]{:S(2)}) copy-start(f32[48,48]{1,0:T(8,128)S(1)} %fusion.118) | copy-start | bytes 27652
  383.3 3.4 copy-start.42
  385.3 3.3 copy-start.58
  399.4 2.1 copy-start.25
  404.2 11.9 %collective-permute-start = (f32[256,384]{1,0:T(8,128)S(1)}, f32[256,384]{1,0:T(8,128)S(1)}, u32[]{:S(2)}, u32[]{:S(2)}) collective-permute-start(f32[256,384]{1,0:T(8,128)S(1)} %broadcast_select_fusion.4), channel_id=1, source_target_pairs={{0,8},{8,0},{16,24},{24,16},{32,40},{40,32},{48,56},{56,48},{64,72... | collective-permute-start | bytes 1179656 | tf_op jit(solution)/shard_map/ppermute | solution.py:16
  407.4 3.0 copy-start.24
  407.4 3.0 copy-start.27
  407.4 3.0 copy-start.39
  407.4 3.0 copy-start.43
  407.4 3.0 copy-start.55
  407.4 3.0 copy-start.59
  407.4 3.0 copy-start.71
  412.2 1.2 copy-start.26
  412.2 1.2 copy-start.28
  413.5 2.6 copy-start.69
  503.4 20.8 %collective-permute-start.1 = (f32[256,384]{1,0:T(8,128)S(1)}, f32[256,384]{1,0:T(8,128)S(1)}, u32[]{:S(2)}, u32[]{:S(2)}) collective-permute-start(f32[256,384]{1,0:T(8,128)S(1)} %broadcast_select_fusion.3), channel_id=1, source_target_pairs={{0,16},{16,0},{8,24},{24,8},{32,48},{48,32},{40,56},{56,40},{64,80... | collective-permute-start | bytes 1179656 | tf_op jit(solution)/shard_map/ppermute | solution.py:16
  612.3 4.9 copy-start.73
  612.4 22.8 %collective-permute-start.2 = (f32[256,384]{1,0:T(8,128)S(1)}, f32[256,384]{1,0:T(8,128)S(1)}, u32[]{:S(2)}, u32[]{:S(2)}) collective-permute-start(f32[256,384]{1,0:T(8,128)S(1)} %broadcast_select_fusion.2), channel_id=1, source_target_pairs={{0,32},{32,0},{8,40},{40,8},{16,48},{48,16},{24,56},{56,24},{64,96... | collective-permute-start | bytes 1179656 | tf_op jit(solution)/shard_map/ppermute | solution.py:16
  723.6 2.3 copy-start.74
  723.7 9.5 %collective-permute-start.3 = (f32[256,384]{1,0:T(8,128)S(1)}, f32[256,384]{1,0:T(8,128)S(1)}, u32[]{:S(2)}, u32[]{:S(2)}) collective-permute-start(f32[256,384]{1,0:T(8,128)S(1)} %broadcast_select_fusion.1), channel_id=1, source_target_pairs={{0,64},{64,0},{8,72},{72,8},{16,80},{80,16},{24,88},{88,24},{32,96... | collective-permute-start | bytes 1179656 | tf_op jit(solution)/shard_map/ppermute | solution.py:16
  821.4 3.8 copy-start.72
  821.5 10.1 %collective-permute-start.4 = (f32[256,384]{1,0:T(8,128)S(1)}, f32[256,384]{1,0:T(8,128)S(1)}, u32[]{:S(2)}, u32[]{:S(2)}) collective-permute-start(f32[256,384]{1,0:T(8,128)S(1)} %broadcast_select_fusion), channel_id=1, source_target_pairs={{0,128},{128,0},{8,136},{136,8},{16,144},{144,16},{24,152},{152,24... | collective-permute-start | bytes 1179656 | tf_op jit(solution)/shard_map/ppermute | solution.py:16
  919.2 3.0 copy-start.1
  (17 other events, 17.0 us)
Sparse Core Ops, SparseCore 0:
  15.4 70.9 all-reduce.57
where the time goes:
time: 944 us; the launch traced here: 929 us
  other arithmetic  633 us (67%)
  matrix products  129 us (14%)
  waiting for transfers between devices  105 us (11%)
  local copies, waits for them, and re-layouts  30.1 us (3%)
  between operations  19.9 us (2%)
  starting transfers between devices  12.5 us (1%)
    another operation x192, other arithmetic, inverse_factor(): lower_factor = jnp.linalg.cholesky(gram_matrix)  331 us
    another operation x128, other arithmetic, inverse_factor(): return jax.scipy.linalg.solve_triangular(lower_factor, identity, lower=True)  283 us
    dot_general x240, matrix products, matmul_high(): jnp.dot(left, right, precision=lax.Precision.HIGHEST, preferred_element_t...  105 us
    psum x1, waiting for transfers between devices, on_device(): summed = lax.psum(partial_value, 'samples')  66.2 us
    ppermute x5, waiting for transfers between devices, partner_2(): return lax.ppermute(block, axis, route)  38.7 us
  transfers between devices with their start and end apart: 6, of which 5 were waited for; matrix products, arithmetic and copies ran while one was open for 3% of the time, Pallas kernels for 0%

commit v1 on v0

v1 whole, which is shorter than its diff:
```python
import functools
import math

import jax
import jax.numpy as jnp
from jax import lax
from jax.experimental import pallas as pl
from jax.experimental.pallas import tpu as pltpu
from jax.sharding import PartitionSpec as P

HIGH = lax.Precision.HIGHEST
NT = (((1,), (1,)), ((), ()))
TN = (((0,), (0,)), ((), ()))
NN = (((1,), (0,)), ((), ()))

def mm(a, b, dims=NN):
    return lax.dot_general(a, b, dims, precision=HIGH, preferred_element_type=jnp.float32)

def row_of(x, i):
    return jnp.broadcast_to(x[:, i:i + 1, :], x.shape)

def eliminate(m_ref):
    batch = m_ref.shape[0]
    shape = (batch, 8, 128)
    sub = lax.broadcasted_iota(jnp.int32, shape, 1)
    lane = lax.broadcasted_iota(jnp.int32, shape, 2)
    zero = jnp.zeros(shape, jnp.float32)
    rows = m_ref[:, 0:8, :]
    for k in range(16):
        lo = 8 * k
        last = k == 15
        in_block = (lane >= lo) & (lane < lo + 8)
        cols = [jnp.broadcast_to(rows[:, :, lo + j:lo + j + 1], shape) for j in range(8)]
        main = jnp.where(in_block, jnp.where(lane - lo == sub, 1.0, 0.0), rows)
        if not last:
            below = m_ref[:, lo + 8:lo + 16, :]
            cols_b = [jnp.broadcast_to(below[:, :, lo + j:lo + j + 1], shape) for j in range(8)]
            nxt = jnp.where(in_block, 0.0, below)
        for j in range(8):
            scale = lax.rsqrt(row_of(cols[j], j))
            left = cols[j] * scale
            if not last:
                left_b = cols_b[j] * scale
            for i in range(j + 1, 8):
                factor = row_of(left, i)
                cols[i] = cols[i] - left * factor
                if not last:
                    cols_b[i] = cols_b[i] - left_b * factor
            pivot_row = row_of(main, j) * scale
            main = jnp.where(sub == j, pivot_row, main - jnp.where(sub > j, left, 0.0) * pivot_row)
            if not last:
                nxt = nxt - left_b * pivot_row
        m_ref[:, lo:lo + 8, :] = main
        if not last:
            rows = nxt
        if k < 14:
            rest = lo + 16
            for b in range(batch):
                panel = main[b]
                upd = lax.dot_general(panel, panel, TN, precision=HIGH, preferred_element_type=jnp.float32)
                keep = m_ref[b, rest:, :]
                lane2 = lax.broadcasted_iota(jnp.int32, keep.shape, 1)
                keep = jnp.where((lane2 >= lo) & (lane2 < lo + 8), 0.0, keep)
                m_ref[b, rest:, :] = keep - upd[rest:, :]

def kern(leaf_ref, stk_ref, up_ref, rows_ref, leaf_o, stk_o, up_o, gram, diag, tinv):
    srcs = (leaf_ref, stk_ref, up_ref)
    for b in range(3):
        w = srcs[b][...]
        for i in range(3):
            g = mm(w[128 * i:128 * i + 128], w[:128 * (i + 1)], NT)
            for j in range(i + 1):
                gram[b, i, j] = g[:, 128 * j:128 * j + 128]
    r = lax.broadcasted_iota(jnp.int32, (128, 128), 0)
    c = lax.broadcasted_iota(jnp.int32, (128, 128), 1)
    @pl.loop(0, 3)
    def _(kk):
        for b in range(3):
            diag[b] = gram[b, kk, kk]
        eliminate(diag)
        for b in range(3):
            tinv[b, kk] = jnp.where(r >= c, diag[b], 0.0)
        @pl.when(kk == 0)
        def _():
            for b in range(3):
                t = tinv[b, 0]
                l10 = mm(gram[b, 1, 0], t, NT)
                l20 = mm(gram[b, 2, 0], t, NT)
                gram[b, 1, 0] = l10
                gram[b, 2, 0] = l20
                gram[b, 1, 1] -= mm(l10, l10, NT)
                gram[b, 2, 1] -= mm(l20, l10, NT)
                gram[b, 2, 2] -= mm(l20, l20, NT)
        @pl.when(kk == 1)
        def _():
            for b in range(3):
                l21 = mm(gram[b, 2, 1], tinv[b, 1], NT)
                gram[b, 2, 1] = l21
                gram[b, 2, 2] -= mm(l21, l21, NT)
    scale = math.sqrt(512)
    outs = (leaf_o, stk_o, up_o)
    for b in range(3):
        t0, t1, t2 = tinv[b, 0], tinv[b, 1], tinv[b, 2]
        l10, l20, l21 = gram[b, 1, 0], gram[b, 2, 0], gram[b, 2, 1]
        i10 = -mm(t1, mm(l10, t0))
        i21 = -mm(t2, mm(l21, t1))
        i20 = -mm(t2, mm(l20, t0) + mm(l21, i10))
        w = rows_ref[...] if b == 0 else srcs[b][...]
        def put(i, inv):
            outs[b][:, 128 * i:128 * i + 128] = lax.dot_general(w[:128 * (i + 1)], inv * scale, (((0,), (1,)), ((), ())), precision=HIGH, preferred_element_type=jnp.float32)
        put(0, t0)
        put(1, jnp.concatenate([i10, t1], 1))
        put(2, jnp.concatenate([i20, i21, t2], 1))

def bases(leaf_t, stk_t, up_t, rows_t):
    vm = pl.BlockSpec(memory_space=pltpu.VMEM)
    return pl.pallas_call(
        kern,
        out_shape=[jax.ShapeDtypeStruct((128, 384), jnp.float32), jax.ShapeDtypeStruct((512, 384), jnp.float32), jax.ShapeDtypeStruct((512, 384), jnp.float32)],
        in_specs=[vm] * 4, out_specs=[vm] * 3,
        scratch_shapes=[pltpu.VMEM((3, 3, 3, 128, 128), jnp.float32), pltpu.VMEM((3, 128, 128), jnp.float32), pltpu.VMEM((3, 3, 128, 128), jnp.float32)],
        compiler_params=pltpu.CompilerParams(vmem_limit_bytes=48 << 20),
        name="bases",
    )(leaf_t, stk_t, up_t, rows_t)


def partner_2(block, axis, bit):
    count = lax.axis_size(axis)
    route = []
    for low in range(count):
        high = low | 1 << bit
        if high != low and high < count:
            route += [(low, high), (high, low)]
    return lax.ppermute(block, axis, route)


def select_rows(matrix_rows, indices):
    return jnp.take(matrix_rows, indices, axis=0)


def climb_tree(current, tree_depth, position, upper_pivots):
    chosen = None
    for height in range(1, tree_depth + 1):
        partner = partner_2(current, "rows", height - 1)
        on_right = position >> height - 1 & 1 == 1
        left_part = jnp.where(on_right, partner, current)
        right_part = jnp.where(on_right, current, partner)
        stacked = jnp.concatenate([left_part, right_part], 0)
        low_bits = position & (1 << height) - 1
        is_owner = low_bits == 1 << height - 1
        if height == tree_depth:
            is_owner = jnp.logical_or(is_owner, position == 0)
        chosen = stacked if chosen is None else jnp.where(is_owner, stacked, chosen)
        if height < tree_depth:
            node_row = (1 << tree_depth - height) + (position >> height) - 2
            indices = lax.dynamic_index_in_dim(upper_pivots, node_row, 0, keepdims=False)
            current = select_rows(stacked, indices)
    return chosen


def on_device(matrix_block, sketch_matrix, local_pivots, upper_pivots):
    partial_value = jnp.dot(matrix_block, sketch_matrix, preferred_element_type=jnp.float32)
    pivots = local_pivots[0]
    summed = lax.psum(partial_value, "samples")
    sample = lax.axis_index("samples")
    own_leaf = lax.dynamic_slice_in_dim(summed, (sample // 4) * 512, 512, 0)
    own_rows = lax.dynamic_slice_in_dim(summed, sample * 128, 128, 0)
    stacked = jnp.concatenate([select_rows(summed[:512], pivots[0]), select_rows(summed[512:], pivots[1])], 0)
    current = select_rows(stacked, pivots[2])
    tree_depth = lax.axis_size("rows").bit_length() - 1
    upper = climb_tree(current, tree_depth, lax.axis_index("rows"), upper_pivots)
    return tuple(bases(own_leaf.T, stacked.T, upper.T, own_rows.T))


def solution(mesh):
    in_specs = (P("rows", "samples"), P("samples", None), P("rows", None, None), P())
    out_specs = (P(("rows", "samples"), None), P("rows", None), P("rows", None))
    return jax.shard_map(
        on_device, mesh=mesh, in_specs=in_specs, out_specs=out_specs, check_vma=False
    )
```

time: 944 us -> 281 us (0.30)
  the two profiles are of different devices: /device:TPU:1 before, /device:TPU:6 now
where the time goes in v1:
time: 281 us; the launch traced here: 280 us
  waiting for transfers between devices  124 us (44%)
  local copies, waits for them, and re-layouts  55.7 us (20%)
  Pallas kernels  35 us (12%)
  other arithmetic  30.9 us (11%)
  starting transfers between devices  14.4 us (5%)
  between operations  14.3 us (5%)
  matrix products  5.88 us (2%)
    psum x1, waiting for transfers between devices, on_device(): summed = lax.psum(partial_value, 'samples')  66 us
    ppermute x5, waiting for transfers between devices, partner_2(): return lax.ppermute(block, axis, route)  57.6 us
    pallas_call x1, Pallas kernels, bases(): pl.pallas_call(kern, out_shape=[jax.ShapeDtypeStruct((128, 384), jnp.floa...  35 us
    gather x14, local copies, waits for them, and re-layouts, select_rows(): return jnp.take(matrix_rows, indices, axis=0)  31.6 us
    ppermute x5, starting transfers between devices, partner_2(): return lax.ppermute(block, axis, route)  14.3 us
    select_n x11, other arithmetic, select_rows(): return jnp.take(matrix_rows, indices, axis=0)  11.7 us
    concatenate x4, local copies, waits for them, and re-layouts, climb_tree(): stacked = jnp.concatenate([left_part, right_part], 0)  9.12 us
    dot_general x1, matrix products, on_device(): jnp.dot(matrix_block, sketch_matrix, preferred_element_type=jnp.float32)  5.88 us
  transfers between devices with their start and end apart: 6, of which 6 were waited for; matrix products, arithmetic and copies ran while one was open for 4% of the time, Pallas kernels for 0%

profile of v1, /device:TPU:6, one launch (start us, length us, event | category | flops | bytes accessed | tf_op | source)
XLA Modules:
  0.0 279.9 jit_solution(9020340303688549037)
XLA Ops:
  7.2 1.5 copy-done
  8.7 5.9 %fusion.4 = f32[1024,384]{0,1:T(8,128)} fusion(bf16[1024,2560]{1,0:T(8,128)(2,1)} %param.6, bf16[2560,384]{1,0:T(8,128)(2,1)S(1)} %copy-done), kind=kOutput, calls=%fused_computation.61 | convolution fusion | flops 2013265920 | bytes 8781824 | tf_op jit(solution)/shard_map/dot_general | solution.py:162
  16.5 0.8 constant_dynamic-slice_fusion
  17.8 0.6 compare_and_fusion.4
  18.4 66.0 %all-reduce.2.cloned.1.call-done = f32[1024,384]{0,1:T(8,128)} async-done(((f32[1024,384]{0,1:T(8,128)}), f32[1024,384]{0,1:T(8,128)}) %all-reduce.2.cloned.1.call-update) | async-done | bytes 1572880 | tf_op jit(solution)/shard_map/psum | solution.py:164
  84.4 2.9 %fusion.2 = (f32[512,384]{0,1:T(8,128)}, f32[512,384]{0,1:T(8,128)}, f32[384,512]{1,0:T(8,128)S(1)}) fusion(f32[1024,384]{0,1:T(8,128)} %all-reduce.2.cloned.1.call-done, s32[]{:T(128)S(6)} %select_n.110), kind=kLoop, calls=%fused_computation.59 | loop fusion | bytes 4718596 | tf_op jit(solution)/shard_map/slice | solution.py:168
  87.4 1.4 copy.8
  88.8 1.9 gather_fusion
  90.7 1.9 copy.9
  92.6 1.4 copy.10
  94.0 1.9 gather_fusion.1
  95.8 1.2 copy.11
  97.0 1.0 broadcast_select_fusion.6
  98.0 0.7 broadcast_select_fusion.5
  98.8 1.1 pad_maximum_fusion
  99.8 2.3 copy.12
  102.1 3.1 %gather_fusion.2 = f32[256,384]{1,0:T(8,128)} fusion(f32[512,384]{1,0:T(8,128)} %copy.12, s32[1024]{0:T(1024)} %pad_clamp_fusion.4), kind=kCustom, calls=%fused_computation.2.clone | custom fusion | bytes 787456 | tf_op jit(solution)/shard_map/jit(_take)/gather | solution.py:138
  105.3 1.9 copy.13
  107.2 1.8 broadcast_select_fusion.4
  108.9 1.6 collective-permute-start
  111.1 1.3 pad_clamp_fusion.3
  113.0 8.1 %collective-permute-done = f32[256,384]{0,1:T(8,128)} collective-permute-done((f32[256,384]{0,1:T(8,128)}, f32[256,384]{0,1:T(8,128)}, u32[]{:S(2)}, u32[]{:S(2)}) %collective-permute-start) | collective-permute-done | bytes 393248 | tf_op jit(solution)/shard_map/ppermute | solution.py:134
  121.0 1.2 broadcast_select_fusion.8
  122.2 0.7 copy-done.1
  123.1 1.0 pad_maximum_fusion.1
  124.1 2.3 copy.14
  126.4 3.1 %gather_fusion.3 = f32[256,384]{1,0:T(8,128)} fusion(f32[512,384]{1,0:T(8,128)} %copy.14, s32[1024]{0:T(1024)} %pad_clamp_fusion.3), kind=kCustom, calls=%fused_computation.3.clone | custom fusion | bytes 787456 | tf_op jit(solution)/shard_map/jit(_take)/gather | solution.py:138
  129.5 1.9 copy.15
  131.4 1.8 broadcast_select_fusion.3
  133.2 2.5 collective-permute-start.1
  135.7 0.7 pad_clamp_fusion.2
  136.4 17.6 %collective-permute-done.1 = f32[256,384]{0,1:T(8,128)} collective-permute-done((f32[256,384]{0,1:T(8,128)}, f32[256,384]{0,1:T(8,128)}, u32[]{:S(2)}, u32[]{:S(2)}) %collective-permute-start.1) | collective-permute-done | bytes 393248 | tf_op jit(solution)/shard_map/ppermute | solution.py:134
  154.0 1.2 broadcast_select_fusion.10
  155.2 0.7 copy-done.5
  156.1 1.0 pad_maximum_fusion.2
  157.1 2.3 copy.16
  159.3 3.0 %gather_fusion.4 = f32[256,384]{1,0:T(8,128)} fusion(f32[512,384]{1,0:T(8,128)} %copy.16, s32[1024]{0:T(1024)S(1)} %pad_clamp_fusion.2), kind=kCustom, calls=%fused_computation.4.clone | custom fusion | bytes 787456 | tf_op jit(solution)/shard_map/jit(_take)/gather | solution.py:138
  162.3 1.9 copy.17
  164.3 1.8 broadcast_select_fusion.2
  166.0 5.7 %collective-permute-start.2 = (f32[256,384]{0,1:T(8,128)}, f32[256,384]{0,1:T(8,128)}, u32[]{:S(2)}, u32[]{:S(2)}) collective-permute-start(f32[256,384]{0,1:T(8,128)} %broadcast_select_fusion.2), channel_id=1, source_target_pairs={{0,32},{32,0},{8,40},{40,8},{16,48},{48,16},{24,56},{56,24},{64,96... | collective-permute-start | bytes 1179656 | tf_op jit(solution)/shard_map/ppermute | solution.py:134
  172.9 16.9 %collective-permute-done.2 = f32[256,384]{0,1:T(8,128)} collective-permute-done((f32[256,384]{0,1:T(8,128)}, f32[256,384]{0,1:T(8,128)}, u32[]{:S(2)}, u32[]{:S(2)}) %collective-permute-start.2) | collective-permute-done | bytes 393248 | tf_op jit(solution)/shard_map/ppermute | solution.py:134
  189.8 1.2 broadcast_select_fusion.12
  191.0 0.7 copy-done.9
  191.9 1.0 pad_maximum_fusion.3
  192.9 2.3 copy.18
  195.2 3.0 %gather_fusion.5 = f32[256,384]{1,0:T(8,128)} fusion(f32[512,384]{1,0:T(8,128)} %copy.18, s32[1024]{0:T(1024)S(1)} %pad_clamp_fusion.1), kind=kCustom, calls=%fused_computation.5.clone | custom fusion | bytes 787456 | tf_op jit(solution)/shard_map/jit(_take)/gather | solution.py:138
  198.2 1.9 copy.19
  200.1 1.8 broadcast_select_fusion.1
  201.9 1.5 collective-permute-start.3
  203.3 0.7 pad_clamp_fusion
  204.0 8.3 %collective-permute-done.3 = f32[256,384]{0,1:T(8,128)} collective-permute-done((f32[256,384]{0,1:T(8,128)}, f32[256,384]{0,1:T(8,128)}, u32[]{:S(2)}, u32[]{:S(2)}) %collective-permute-start.3) | collective-permute-done | bytes 393248 | tf_op jit(solution)/shard_map/ppermute | solution.py:134
  212.3 1.2 broadcast_select_fusion.14
  213.5 0.7 copy-done.12
  214.3 1.0 pad_maximum_fusion.4
  215.3 2.3 copy.20
  217.6 3.0 %gather_fusion.6 = f32[256,384]{1,0:T(8,128)} fusion(f32[512,384]{1,0:T(8,128)} %copy.20, s32[1024]{0:T(1024)S(1)} %pad_clamp_fusion), kind=kCustom, calls=%fused_computation.6.clone | custom fusion | bytes 787456 | tf_op jit(solution)/shard_map/jit(_take)/gather | solution.py:138
  220.6 1.9 copy.21
  222.5 1.8 broadcast_select_fusion
  224.3 3.0 %collective-permute-start.4 = (f32[256,384]{0,1:T(8,128)}, f32[256,384]{0,1:T(8,128)}, u32[]{:S(2)}, u32[]{:S(2)}) collective-permute-start(f32[256,384]{0,1:T(8,128)} %broadcast_select_fusion), channel_id=1, source_target_pairs={{0,128},{128,0},{8,136},{136,8},{16,144},{144,16},{24,152},{152,24... | collective-permute-start | bytes 1179656 | tf_op jit(solution)/shard_map/ppermute | solution.py:134
  227.3 1.1 dynamic-slice_bitcast_fusion.1.rows_ref
  228.4 6.9 %collective-permute-done.4 = f32[256,384]{0,1:T(8,128)} collective-permute-done((f32[256,384]{0,1:T(8,128)}, f32[256,384]{0,1:T(8,128)}, u32[]{:S(2)}, u32[]{:S(2)}) %collective-permute-start.4) | collective-permute-done | bytes 393248 | tf_op jit(solution)/shard_map/ppermute | solution.py:134
  235.3 1.2 broadcast_select_fusion.16
  236.5 1.5 fusion.up_ref
  238.1 35.0 %bases.1 = (f32[128,384]{1,0:T(8,128)}, f32[512,384]{1,0:T(8,128)}, f32[512,384]{1,0:T(8,128)}) custom-call(f32[384,512]{1,0:T(8,128)S(1)} %get-tuple-element.6.leaf_ref, f32[384,512]{1,0:T(8,128)S(1)} %get-tuple-element.18.stk_ref, f32[384,512]{1,0:T(8,128)S(1)} %fusion.up_ref, f32[384,128]{1,0:T(8,128)S(1)} %dynamic-slice_bitcast_fusion.1.rows_ref), custom_call_target="tpu_custom_call" | custom-call | tf_op jit(solution)/shard_map/bases/pallas_call | solution.py:117
  (45 shorter events, 5.4 us)
Async XLA Ops:
  7.2 1.6 copy-start
  7.2 7.5 %copy-start.17 = (s32[1,3,256]{2,0,1:T(1,128)S(1)}, s32[1,3,256]{2,0,1:T(1,128)}, u32[]{:S(2)}) copy-start(s32[1,3,256]{2,0,1:T(1,128)} %param.8) | copy-start | bytes 9220
  7.2 77.3 %all-reduce.2.cloned.1.call-start = ((), (), s32[]{:S(2)}) async-start(), calls=%async_computation | async-start | bytes 3145728 | tf_op jit(solution)/shard_map/psum | solution.py:164
  108.9 12.1 %collective-permute-start = (f32[256,384]{0,1:T(8,128)}, f32[256,384]{0,1:T(8,128)}, u32[]{:S(2)}, u32[]{:S(2)}) collective-permute-start(f32[256,384]{0,1:T(8,128)} %broadcast_select_fusion.4), channel_id=1, source_target_pairs={{0,8},{8,0},{16,24},{24,16},{32,40},{40,32},{48,56},{56,48},{64,72... | collective-permute-start | bytes 1179656 | tf_op jit(solution)/shard_map/ppermute | solution.py:134
  122.2 0.7 copy-start.1
  122.2 0.9 copy-start.3
  126.4 5.1 %copy-start.15 = (pred[256]{0:T(512)(128)(4,1)S(1)}, pred[256]{0:T(512)(128)(4,1)}, u32[]{:S(2)}) copy-start(pred[256]{0:T(512)(128)(4,1)} %get-tuple-element.35) | copy-start | bytes 772
  133.2 20.8 %collective-permute-start.1 = (f32[256,384]{0,1:T(8,128)}, f32[256,384]{0,1:T(8,128)}, u32[]{:S(2)}, u32[]{:S(2)}) collective-permute-start(f32[256,384]{0,1:T(8,128)} %broadcast_select_fusion.3), channel_id=1, source_target_pairs={{0,16},{16,0},{8,24},{24,8},{32,48},{48,32},{40,56},{56,40},{64,80... | collective-permute-start | bytes 1179656 | tf_op jit(solution)/shard_map/ppermute | solution.py:134
  155.2 0.8 copy-start.5
  155.2 0.9 copy-start.7
  159.3 4.9 %copy-start.14 = (pred[256]{0:T(512)(128)(4,1)S(1)}, pred[256]{0:T(512)(128)(4,1)}, u32[]{:S(2)}) copy-start(pred[256]{0:T(512)(128)(4,1)} %get-tuple-element.34) | copy-start | bytes 772
  166.0 23.8 %collective-permute-start.2 = (f32[256,384]{0,1:T(8,128)}, f32[256,384]{0,1:T(8,128)}, u32[]{:S(2)}, u32[]{:S(2)}) collective-permute-start(f32[256,384]{0,1:T(8,128)} %broadcast_select_fusion.2), channel_id=1, source_target_pairs={{0,32},{32,0},{8,40},{40,8},{16,48},{48,16},{24,56},{56,24},{64,96... | collective-permute-start | bytes 1179656 | tf_op jit(solution)/shard_map/ppermute | solution.py:134
  191.0 0.8 copy-start.9
  191.0 0.9 copy-start.11
  195.2 4.9 %copy-start.16 = (pred[256]{0:T(512)(128)(4,1)S(1)}, pred[256]{0:T(512)(128)(4,1)}, u32[]{:S(2)}) copy-start(pred[256]{0:T(512)(128)(4,1)} %get-tuple-element.33) | copy-start | bytes 772
  201.9 10.4 %collective-permute-start.3 = (f32[256,384]{0,1:T(8,128)}, f32[256,384]{0,1:T(8,128)}, u32[]{:S(2)}, u32[]{:S(2)}) collective-permute-start(f32[256,384]{0,1:T(8,128)} %broadcast_select_fusion.1), channel_id=1, source_target_pairs={{0,64},{64,0},{8,72},{72,8},{16,80},{80,16},{24,88},{88,24},{32,96... | collective-permute-start | bytes 1179656 | tf_op jit(solution)/shard_map/ppermute | solution.py:134
  213.5 0.8 copy-start.12
  213.5 0.9 copy-start.13
  224.3 11.0 %collective-permute-start.4 = (f32[256,384]{0,1:T(8,128)}, f32[256,384]{0,1:T(8,128)}, u32[]{:S(2)}, u32[]{:S(2)}) collective-permute-start(f32[256,384]{0,1:T(8,128)} %broadcast_select_fusion), channel_id=1, source_target_pairs={{0,128},{128,0},{8,136},{136,8},{16,144},{144,16},{24,152},{152,24... | collective-permute-start | bytes 1179656 | tf_op jit(solution)/shard_map/ppermute | solution.py:134
  227.3 9.2 %copy-start.2 = (f32[256,384]{0,1:T(8,128)S(1)}, f32[256,384]{0,1:T(8,128)}, u32[]{:S(2)}) copy-start(f32[256,384]{0,1:T(8,128)} %copy-done.1) | copy-start | bytes 1179652
  227.3 9.2 %copy-start.4 = (f32[256,384]{0,1:T(8,128)S(1)}, f32[256,384]{0,1:T(8,128)}, u32[]{:S(2)}) copy-start(f32[256,384]{0,1:T(8,128)} %copy-done.3) | copy-start | bytes 1179652
  227.3 9.2 %copy-start.6 = (f32[256,384]{0,1:T(8,128)S(1)}, f32[256,384]{0,1:T(8,128)}, u32[]{:S(2)}) copy-start(f32[256,384]{0,1:T(8,128)} %copy-done.5) | copy-start | bytes 1179652
  227.3 9.2 %copy-start.8 = (f32[256,384]{0,1:T(8,128)S(1)}, f32[256,384]{0,1:T(8,128)}, u32[]{:S(2)}) copy-start(f32[256,384]{0,1:T(8,128)} %copy-done.7) | copy-start | bytes 1179652
  227.3 9.2 %copy-start.10 = (f32[256,384]{0,1:T(8,128)S(1)}, f32[256,384]{0,1:T(8,128)}, u32[]{:S(2)}) copy-start(f32[256,384]{0,1:T(8,128)} %copy-done.9) | copy-start | bytes 1179652
Sparse Core Ops, SparseCore 0:
  14.7 69.6 all-reduce.1

commit v2 on v1

--- a/solution.py
+++ b/solution.py
@@ -63,7 +63,7 @@
                 keep = jnp.where((lane2 >= lo) & (lane2 < lo + 8), 0.0, keep)
                 m_ref[b, rest:, :] = keep - upd[rest:, :]
 
-def kern(leaf_ref, stk_ref, up_ref, rows_ref, leaf_o, stk_o, up_o, gram, diag, tinv):
+def kern(leaf_ref, stk_ref, up_ref, leaf_o, stk_o, up_o, gram, diag, tinv):
     srcs = (leaf_ref, stk_ref, up_ref)
     for b in range(3):
         w = srcs[b][...]
@@ -98,6 +98,7 @@
                 gram[b, 2, 1] = l21
                 gram[b, 2, 2] -= mm(l21, l21, NT)
     scale = math.sqrt(512)
+    share = pl.ds(pl.multiple_of((lax.axis_index("samples") % 4) * 128, 128), 128)
     outs = (leaf_o, stk_o, up_o)
     for b in range(3):
         t0, t1, t2 = tinv[b, 0], tinv[b, 1], tinv[b, 2]
@@ -105,71 +106,252 @@
         i10 = -mm(t1, mm(l10, t0))
         i21 = -mm(t2, mm(l21, t1))
         i20 = -mm(t2, mm(l20, t0) + mm(l21, i10))
-        w = rows_ref[...] if b == 0 else srcs[b][...]
+        w = leaf_ref[:, share] if b == 0 else srcs[b][...]
         def put(i, inv):
             outs[b][:, 128 * i:128 * i + 128] = lax.dot_general(w[:128 * (i + 1)], inv * scale, (((0,), (1,)), ((), ())), precision=HIGH, preferred_element_type=jnp.float32)
         put(0, t0)
         put(1, jnp.concatenate([i10, t1], 1))
         put(2, jnp.concatenate([i20, i21, t2], 1))
 
-def bases(leaf_t, stk_t, up_t, rows_t):
+def bases(leaf_t, stk_t, up_t):
     vm = pl.BlockSpec(memory_space=pltpu.VMEM)
     return pl.pallas_call(
         kern,
         out_shape=[jax.ShapeDtypeStruct((128, 384), jnp.float32), jax.ShapeDtypeStruct((512, 384), jnp.float32), jax.ShapeDtypeStruct((512, 384), jnp.float32)],
-        in_specs=[vm] * 4, out_specs=[vm] * 3,
+        in_specs=[vm] * 3, out_specs=[vm] * 3,
         scratch_shapes=[pltpu.VMEM((3, 3, 3, 128, 128), jnp.float32), pltpu.VMEM((3, 128, 128), jnp.float32), pltpu.VMEM((3, 3, 128, 128), jnp.float32)],
         compiler_params=pltpu.CompilerParams(vmem_limit_bytes=48 << 20),
         name="bases",
-    )(leaf_t, stk_t, up_t, rows_t)
-
-
-def partner_2(block, axis, bit):
-    count = lax.axis_size(axis)
-    route = []
-    for low in range(count):
-        high = low | 1 << bit
-        if high != low and high < count:
-            route += [(low, high), (high, low)]
-    return lax.ppermute(block, axis, route)
-
-
-def select_rows(matrix_rows, indices):
-    return jnp.take(matrix_rows, indices, axis=0)
-
-
-def climb_tree(current, tree_depth, position, upper_pivots):
-    chosen = None
-    for height in range(1, tree_depth + 1):
-        partner = partner_2(current, "rows", height - 1)
-        on_right = position >> height - 1 & 1 == 1
-        left_part = jnp.where(on_right, partner, current)
-        right_part = jnp.where(on_right, current, partner)
-        stacked = jnp.concatenate([left_part, right_part], 0)
-        low_bits = position & (1 << height) - 1
-        is_owner = low_bits == 1 << height - 1
-        if height == tree_depth:
-            is_owner = jnp.logical_or(is_owner, position == 0)
-        chosen = stacked if chosen is None else jnp.where(is_owner, stacked, chosen)
-        if height < tree_depth:
-            node_row = (1 << tree_depth - height) + (position >> height) - 2
-            indices = lax.dynamic_index_in_dim(upper_pivots, node_row, 0, keepdims=False)
-            current = select_rows(stacked, indices)
-    return chosen
+    )(leaf_t, stk_t, up_t)
+
+
+MESH = pl.DeviceIdType.MESH
+SHARE = 48
+HALF = 192
+
+
+def pick(values, indices):
+    high = values.astype(jnp.bfloat16)
+    rest = values - high.astype(jnp.float32)
+    middle = rest.astype(jnp.bfloat16)
+    low = (rest - middle.astype(jnp.float32)).astype(jnp.bfloat16)
+    terms = jnp.concatenate([high, middle, low], 0)
+    rows = lax.broadcasted_iota(jnp.int32, (values.shape[1], indices.shape[1]), 0)
+    chosen = jnp.where(rows == indices, 1.0, 0.0).astype(jnp.bfloat16)
+    found = jnp.dot(terms, chosen, preferred_element_type=jnp.float32)
+    count = values.shape[0]
+    return found[:count] + found[count:2 * count] + found[2 * count:]
+
+
+def exchange(pt_ref, piv_ref, node_ref, leaf_ref, stk_ref, up_ref,
+             swap, half_sum, parts, own, own_stk, below, climb_in, climb_out,
+             swap_send, swap_recv, part_send, part_recv, gather_send, gather_recv,
+             pair_send, pair_recv, tree_send, tree_recv):
+    r = lax.axis_index("rows")
+    s = lax.axis_index("samples")
+    x = s // 2
+    c = s % 2
+    twin = s + 1 - 2 * c
+    level2 = (r % 4) == 2
+    level3 = (r % 8) == 4
+    level4 = (r % 16) == 8
+    odd = (r % 2) == 1
+    root = (r % 16) == 0
+
+    def peer(d):
+        return ((x + d) % 4) * 2 + c
+
+    def at(row, sample):
+        return (row, sample)
+
+    barrier = pltpu.get_barrier_semaphore()
+
+    def greet(row, sample):
+        pl.semaphore_signal(barrier, inc=1, device_id=at(row, sample), device_id_type=MESH)
+
+    greet(r, twin)
+    for d in range(1, 4):
+        greet(r, peer(d))
+    step = jnp.where(level2, 1, jnp.where(level3, 2, jnp.where(level4, 4, 8)))
+
+    @pl.when(odd)
+    def _():
+        greet(r - 1, s)
+
+    @pl.when(jnp.logical_not(odd))
+    def _():
+        greet(jnp.where(r == 0, 8, r - step), s)
+        greet(jnp.where(r == 0, 24, r + step), s)
+
+    even = jnp.where(odd, 0, 1)
+    pl.semaphore_wait(barrier, 4 + even + jnp.where(root, 0, 1) + jnp.where(level4, 1, 0))
+
+    def swap_copy(h):
+        return pltpu.make_async_remote_copy(
+            src_ref=pt_ref.at[pl.ds(pl.multiple_of(HALF * (1 - c), 8), HALF), pl.ds(512 * h, 512)],
+            dst_ref=swap.at[h],
+            send_sem=swap_send.at[h], recv_sem=swap_recv.at[h],
+            device_id=at(r, twin), device_id_type=MESH)
+
+    swap_copy(0).start()
+    swap_copy(1).start()
+
+    def part_copy(h, d):
+        return pltpu.make_async_remote_copy(
+            src_ref=half_sum.at[h, pl.ds(pl.multiple_of(SHARE * ((x + d) % 4), 8), SHARE), :],
+            dst_ref=parts.at[h, d - 1],
+            send_sem=part_send.at[h, d - 1], recv_sem=part_recv.at[h, d - 1],
+            device_id=at(r, peer(d)), device_id_type=MESH)
+
+    for h in range(2):
+        swap_copy(h).wait_recv()
+        half_sum[h] = pt_ref[pl.ds(pl.multiple_of(HALF * c, 8), HALF), 512 * h:512 * h + 512] + swap[h]
+        for d in (2, 1, 3):
+            part_copy(h, d).start()
+    my_rows = pl.ds(pl.multiple_of(SHARE * x, 8), SHARE)
+    my_place = pl.ds(pl.multiple_of(HALF * c + SHARE * x, 8), SHARE)
+    my_half = pl.ds(pl.multiple_of(HALF * c, 8), HALF)
+
+    def gather_copy(n, d):
+        out = (leaf_ref, stk_ref, up_ref)[n]
+        src = (own.at[((x + d) % 4) // 2], own_stk, climb_in)[n]
+        return pltpu.make_async_remote_copy(
+            src_ref=src, dst_ref=out.at[my_place, :],
+            send_sem=gather_send.at[n, d - 1], recv_sem=gather_recv.at[n, d - 1],
+            device_id=at(r, peer(d)), device_id_type=MESH)
+
+    def pair_copy(n):
+        out = (leaf_ref, stk_ref, up_ref)[n]
+        return pltpu.make_async_remote_copy(
+            src_ref=out.at[my_half, :], dst_ref=out.at[my_half, :],
+            send_sem=pair_send.at[n], recv_sem=pair_recv.at[n],
+            device_id=at(r, twin), device_id_type=MESH)
+
+    for h in range(2):
+        for d in (1, 3, 2):
+            part_copy(h, d).wait_recv()
+        total = half_sum[h, my_rows, :] + parts[h, 0] + parts[h, 1] + parts[h, 2]
+        own[h] = total
+        own_stk[:, 256 * h:256 * h + 256] = pick(total, piv_ref[h:h + 1, :])
+    stacked = own_stk[...]
+    skeleton = pick(stacked, piv_ref[2:3, :])
+
+    def skeleton_copy():
+        return pltpu.make_async_remote_copy(
+            src_ref=below, dst_ref=climb_in.at[:, pl.ds(0, 256)],
+            send_sem=tree_send.at[0], recv_sem=tree_recv.at[0],
+            device_id=at(r + 1, s), device_id_type=MESH)
+
+    @pl.when(odd)
+    def _():
+        climb_in[:, 256:] = skeleton
+
+    @pl.when(jnp.logical_not(odd))
+    def _():
+        below[...] = skeleton
+        skeleton_copy().start()
+
+    leaf_ref[my_place, :] = own[x // 2]
+    stk_ref[my_place, :] = stacked
+    for n in range(2):
+        for d in (2, 1, 3):
+            gather_copy(n, d).start()
+
+    width = jnp.where(odd, 2, 2 * (2 * step))
+    side = (r // width) % 2
+    reach = width // 2
+    parent = jnp.where(side == 0, r + reach, r - reach)
+
+    def tree_copy(to, sem):
+        return pltpu.make_async_remote_copy(
+            src_ref=climb_out,
+            dst_ref=climb_in.at[:, pl.ds(pl.multiple_of(256 * side, 128), 256)],
+            send_sem=tree_send.at[sem], recv_sem=tree_recv.at[side],
+            device_id=at(to, s), device_id_type=MESH)
+
+    def arrived(half):
+        return pltpu.make_async_remote_copy(
+            src_ref=climb_out, dst_ref=climb_in.at[:, pl.ds(256 * half, 256)],
+            send_sem=tree_send.at[1], recv_sem=tree_recv.at[half],
+            device_id=at(r, twin), device_id_type=MESH)
+
+    arrived(0).wait_recv()
+
+    @pl.when(jnp.logical_not(odd))
+    def _():
+        arrived(1).wait_recv()
+
+    @pl.when(jnp.logical_not(root))
+    def _():
+        climb_out[...] = pick(climb_in[...], node_ref[...])
+        tree_copy(parent, 1).start()
+
+    @pl.when(level4)
+    def _():
+        tree_copy(0, 2).start()
+
+    up_ref[my_place, :] = climb_in[...]
+    for d in (2, 1, 3):
+        gather_copy(2, d).start()
+    for n in range(3):
+        for d in (1, 3, 2):
+            gather_copy(n, d).wait_recv()
+        pair_copy(n).start()
+    for h in range(2):
+        swap_copy(h).wait_send()
+        for d in range(1, 4):
+            part_copy(h, d).wait_send()
+    for n in range(3):
+        for d in range(1, 4):
+            gather_copy(n, d).wait_send()
+
+    @pl.when(jnp.logical_not(odd))
+    def _():
+        skeleton_copy().wait_send()
+
+    @pl.when(jnp.logical_not(root))
+    def _():
+        tree_copy(parent, 1).wait_send()
+
+    @pl.when(level4)
+    def _():
+        tree_copy(0, 2).wait_send()
+
+    for n in range(3):
+        pair_copy(n).wait()
+
+
+def gathered(partial_t, pivots, node_pivots):
+    vmem = pl.BlockSpec(memory_space=pltpu.VMEM)
+    f32 = jnp.float32
+    dma = pltpu.SemaphoreType.DMA
+    return pl.pallas_call(
+        exchange,
+        out_shape=[jax.ShapeDtypeStruct((384, 512), f32)] * 3,
+        in_specs=[vmem] * 3, out_specs=[vmem] * 3,
+        scratch_shapes=[
+            pltpu.VMEM((2, HALF, 512), f32), pltpu.VMEM((2, HALF, 512), f32),
+            pltpu.VMEM((2, 3, SHARE, 512), f32), pltpu.VMEM((2, SHARE, 512), f32),
+            pltpu.VMEM((SHARE, 512), f32), pltpu.VMEM((SHARE, 256), f32),
+            pltpu.VMEM((SHARE, 512), f32), pltpu.VMEM((SHARE, 256), f32),
+            dma((2,)), dma((2,)), dma((2, 3)), dma((2, 3)), dma((3, 3)), dma((3, 3)),
+            dma((3,)), dma((3,)), dma((3,)), dma((2,)),
+        ],
+        compiler_params=pltpu.CompilerParams(collective_id=0, has_side_effects=True, vmem_limit_bytes=48 << 20),
+        name="exchange",
+    )(partial_t, pivots, node_pivots)
 
 
 def on_device(matrix_block, sketch_matrix, local_pivots, upper_pivots):
-    partial_value = jnp.dot(matrix_block, sketch_matrix, preferred_element_type=jnp.float32)
-    pivots = local_pivots[0]
-    summed = lax.psum(partial_value, "samples")
-    sample = lax.axis_index("samples")
-    own_leaf = lax.dynamic_slice_in_dim(summed, (sample // 4) * 512, 512, 0)
-    own_rows = lax.dynamic_slice_in_dim(summed, sample * 128, 128, 0)
-    stacked = jnp.concatenate([select_rows(summed[:512], pivots[0]), select_rows(summed[512:], pivots[1])], 0)
-    current = select_rows(stacked, pivots[2])
-    tree_depth = lax.axis_size("rows").bit_length() - 1
-    upper = climb_tree(current, tree_depth, lax.axis_index("rows"), upper_pivots)
-    return tuple(bases(own_leaf.T, stacked.T, upper.T, own_rows.T))
+    partial_t = lax.dot_general(
+        sketch_matrix, matrix_block, (((0,), (1,)), ((), ())), preferred_element_type=jnp.float32)
+    table = []
+    for r in range(32):
+        level = 5 if r == 0 else (r & -r).bit_length()
+        table.append(0 if level == 5 else 2 ** (5 - level) + (r >> level) - 2)
+    node_row = jnp.asarray(table, jnp.int32)[lax.axis_index("rows")]
+    node_pivots = lax.dynamic_slice_in_dim(upper_pivots, node_row, 1, 0)
+    return tuple(bases(*gathered(partial_t, local_pivots[0], node_pivots)))
 
 
 def solution(mesh):

time: 281 us -> 94.8 us (0.34)
  the two profiles are of different devices: /device:TPU:6 before, /device:TPU:1 now
where the time goes in v2:
time: 94.8 us; the launch traced here: 94.6 us
  Pallas kernels  84.5 us (89%)
  matrix products  4.73 us (5%)
  local copies, waits for them, and re-layouts  2.78 us (3%)
  between operations  2.6 us (3%)
    pallas_call x1, Pallas kernels, gathered(): pl.pallas_call(exchange, out_shape=[jax.ShapeDtypeStruct((384, 512), f32)...  49.5 us
    pallas_call x1, Pallas kernels, bases(): pl.pallas_call(kern, out_shape=[jax.ShapeDtypeStruct((128, 384), jnp.floa...  35 us
    dot_general x1, matrix products, on_device(): lax.dot_general(sketch_matrix, matrix_block, (((0,), (1,)), ((), ())), pr...  4.73 us

profile of v2, /device:TPU:1, one launch (start us, length us, event | category | flops | bytes accessed | tf_op | source)
XLA Modules:
  0.0 94.6 jit_solution(10642512335378309626)
XLA Ops:
  0.6 0.0 copy-start
  0.6 1.4 %dynamic_slice.6 = s32[1]{0:T(128)} dynamic-slice(s32[32]{0:T(128)} %constant.14.clone, s32[]{:T(128)S(6)} %select_n.6), dynamic_slice_sizes={1} | dynamic-slice | bytes 12 | tf_op jit(solution)/shard_map/dynamic_slice | solution.py:352
  4.0 0.7 constant_dynamic-slice_fusion.node_ref
  4.7 0.7 copy.10
  5.4 0.0 copy-done
  5.4 4.7 %fusion.pt_ref = f32[384,1024]{1,0:T(8,128)S(1)} fusion(bf16[2560,384]{1,0:T(8,128)(2,1)S(1)} %copy-done, bf16[1024,2560]{1,0:T(8,128)(2,1)} %param.5), kind=kOutput, calls=%fused_computation.2 | convolution fusion | flops 2013265920 | bytes 8781824 | tf_op jit(solution)/shard_map/dot_general | solution.py:346
  10.1 49.5 %exchange.1 = (f32[384,512]{1,0:T(8,128)S(1)}, f32[384,512]{1,0:T(8,128)S(1)}, f32[384,512]{1,0:T(8,128)S(1)}) custom-call(f32[384,1024]{1,0:T(8,128)S(1)} %fusion.pt_ref, s32[3,256]{1,0:T(4,128)S(1)} %bitcast.6, s32[1,256]{1,0:T(1,128)S(1)} %constant_dynamic-slice_fusion.node_ref), custom_call_target="tpu_custom_call" | custom-call | tf_op jit(solution)/shard_map/exchange/pallas_call | solution.py:328
  59.6 35.0 %bases.1 = (f32[128,384]{1,0:T(8,128)}, f32[512,384]{1,0:T(8,128)}, f32[512,384]{1,0:T(8,128)}) custom-call(f32[384,512]{1,0:T(8,128)S(1)} %get-tuple-element.6.leaf_ref, f32[384,512]{1,0:T(8,128)S(1)} %get-tuple-element.7.stk_ref, f32[384,512]{1,0:T(8,128)S(1)} %get-tuple-element.8.up_ref), custom_call_target="tpu_custom_call" | custom-call | tf_op jit(solution)/shard_map/bases/pallas_call | solution.py:118
Async XLA Ops:
  0.6 4.7 %copy-start = (bf16[2560,384]{1,0:T(8,128)(2,1)S(1)}, bf16[2560,384]{1,0:T(8,128)(2,1)}, u32[]{:S(2)}) copy-start(bf16[2560,384]{1,0:T(8,128)(2,1)} %param.6) | copy-start | bytes 5898244

commit v3 on v0

v3 whole, which is shorter than its diff:
```python
import math

import jax
import jax.numpy as jnp
from jax import lax
from jax.experimental import pallas as pl
from jax.experimental.pallas import tpu as pltpu
from jax.sharding import PartitionSpec as P

SUBS = 4
NN = (((1,), (0,)), ((), ()))
NT = (((1,), (1,)), ((), ()))
TN = (((0,), (0,)), ((), ()))
TT = (((0,), (1,)), ((), ()))

def mm(a, b, dims):
    return lax.dot_general(a, b, dims, precision=lax.Precision.HIGH, preferred_element_type=jnp.float32)

def row_of(x, i):
    return jnp.broadcast_to(x[:, i:i + 1, :], x.shape)

def eliminate(m_ref):
    batch = m_ref.shape[0]
    shape = (batch, 8, 128)
    sub = lax.broadcasted_iota(jnp.int32, shape, 1)
    lane = lax.broadcasted_iota(jnp.int32, shape, 2)
    span = 8 * SUBS
    for start in range(0, 128, span):
        groups = [m_ref[:, start + 8 * g:start + 8 * g + 8, :] for g in range(SUBS)]
        for q in range(SUBS):
            lo = start + 8 * q
            in_block = (lane >= lo) & (lane < lo + 8)
            cols = [None] * q + [[jnp.broadcast_to(groups[g][:, :, lo + j:lo + j + 1], shape) for j in range(8)] for g in range(q, SUBS)]
            groups[q] = jnp.where(in_block, jnp.where(lane - lo == sub, 1.0, 0.0), groups[q])
            for g in range(q + 1, SUBS):
                groups[g] = jnp.where(in_block, 0.0, groups[g])
            pivot = row_of(cols[q][0], 0)
            for j in range(8):
                scale = lax.rsqrt(pivot)
                inverse = scale * scale
                own = cols[q]
                column = own[j]
                if j < 7:
                    raw = row_of(column, j + 1)
                    pivot = row_of(own[j + 1], j + 1) - (raw * raw) * inverse
                for i in range(j + 1, 8):
                    factor = row_of(column, i) * inverse
                    for g in range(q, SUBS):
                        cols[g][i] = cols[g][i] - cols[g][j] * factor
                base = row_of(groups[q], j)
                scaled = base * inverse
                groups[q] = jnp.where(sub == j, base * scale, groups[q] - jnp.where(sub > j, column, 0.0) * scaled)
                for g in range(q + 1, SUBS):
                    groups[g] = groups[g] - cols[g][j] * scaled
        for g in range(SUBS):
            m_ref[:, start + 8 * g:start + 8 * g + 8, :] = groups[g]
        rest = start + span
        if rest < 128:
            for b in range(batch):
                panel = jnp.concatenate([groups[g][b] for g in range(SUBS)], 0)
                prow = lax.broadcasted_iota(jnp.int32, panel.shape, 0)
                plane = lax.broadcasted_iota(jnp.int32, panel.shape, 1)
                done = jnp.where((plane >= start) & (plane < rest) & (plane - start >= (prow // 8) * 8 + 8), 0.0, panel)
                upd = mm(panel, done, TN)
                keep = m_ref[b, rest:, :]
                lane2 = lax.broadcasted_iota(jnp.int32, keep.shape, 1)
                keep = jnp.where((lane2 >= start) & (lane2 < rest), 0.0, keep)
                m_ref[b, rest:, :] = keep - upd[rest:, :]

def factor(leaf_ref, stk_ref, up_ref, leaf_o, stk_o, up_o, diag):
    srcs = (leaf_ref, stk_ref, up_ref)
    outs = (leaf_o, stk_o, up_o)
    share = pl.ds(pl.multiple_of((lax.axis_index("samples") % 4) * 128, 128), 128)
    r = lax.broadcasted_iota(jnp.int32, (128, 128), 0)
    c = lax.broadcasted_iota(jnp.int32, (128, 128), 1)
    lower = r >= c
    scale = math.sqrt(512)
    def blk(b, i):
        return srcs[b][128 * i:128 * i + 128, :]
    def rows(b, i):
        return leaf_ref[128 * i:128 * i + 128, share] if b == 0 else blk(b, i)
    B = range(3)
    for b in B:
        diag[0, b] = mm(blk(b, 0), blk(b, 0), NT)
    g10 = [mm(blk(b, 1), blk(b, 0), NT) for b in B]
    g20 = [mm(blk(b, 2), blk(b, 0), NT) for b in B]
    g11 = [mm(blk(b, 1), blk(b, 1), NT) for b in B]
    g21 = [mm(blk(b, 2), blk(b, 1), NT) for b in B]
    g22 = [mm(blk(b, 2), blk(b, 2), NT) for b in B]
    eliminate(diag.at[0])
    t0 = [jnp.where(lower, diag[0, b], 0.0) for b in B]
    l10 = [mm(g10[b], t0[b], NT) for b in B]
    for b in B:
        diag[1, b] = g11[b] - mm(l10[b], l10[b], NT)
    l20 = [mm(g20[b], t0[b], NT) for b in B]
    g21 = [g21[b] - mm(l20[b], l10[b], NT) for b in B]
    g22 = [g22[b] - mm(l20[b], l20[b], NT) for b in B]
    x0 = [mm(rows(b, 0), t0[b] * scale, TT) for b in B]
    for b in B:
        outs[b][:, :128] = x0[b]
    l10s = [l10[b] * (1 / scale) for b in B]
    l20s = [l20[b] * (1 / scale) for b in B]
    y1 = [rows(b, 1).T - mm(x0[b], l10s[b], NT) for b in B]
    y2 = [rows(b, 2).T - mm(x0[b], l20s[b], NT) for b in B]
    eliminate(diag.at[1])
    t1 = [jnp.where(lower, diag[1, b], 0.0) for b in B]
    l21 = [mm(g21[b], t1[b], NT) for b in B]
    for b in B:
        diag[2, b] = g22[b] - mm(l21[b], l21[b], NT)
    x1 = [mm(y1[b], t1[b] * scale, NT) for b in B]
    for b in B:
        outs[b][:, 128:256] = x1[b]
    y2 = [y2[b] - mm(x1[b], l21[b] * (1 / scale), NT) for b in B]
    eliminate(diag.at[2])
    t2 = [jnp.where(lower, diag[2, b], 0.0) for b in B]
    for b in B:
        outs[b][:, 256:] = mm(y2[b], t2[b] * scale, NT)

def bases(leaf_t, stk_t, up_t):
    vm = pl.BlockSpec(memory_space=pltpu.VMEM)
    f32 = jnp.float32
    return pl.pallas_call(
        factor,
        out_shape=[jax.ShapeDtypeStruct((128, 384), f32), jax.ShapeDtypeStruct((512, 384), f32), jax.ShapeDtypeStruct((512, 384), f32)],
        in_specs=[vm] * 3, out_specs=[vm] * 3,
        scratch_shapes=[pltpu.VMEM((3, 3, 128, 128), f32)],
        compiler_params=pltpu.CompilerParams(vmem_limit_bytes=48 << 20),
        name="bases",
    )(leaf_t, stk_t, up_t)


MESH = pl.DeviceIdType.MESH
SHARE = 48
HALF = 192
PART = 24


def pick(values, indices):
    high = values.astype(jnp.bfloat16)
    rest = values - high.astype(jnp.float32)
    middle = rest.astype(jnp.bfloat16)
    low = (rest - middle.astype(jnp.float32)).astype(jnp.bfloat16)
    terms = jnp.concatenate([high, middle, low], 0)
    rows = lax.broadcasted_iota(jnp.int32, (values.shape[1], indices.shape[1]), 0)
    chosen = jnp.where(rows == indices, 1.0, 0.0).astype(jnp.bfloat16)
    found = jnp.dot(terms, chosen, preferred_element_type=jnp.float32)
    count = values.shape[0]
    return found[:count] + found[count:2 * count] + found[2 * count:]


def exchange(pt_ref, piv_ref, node_ref, leaf_ref, stk_ref, up_ref,
             swap, half_sum, passing, parts, own, own_stk, below, climb_in, climb_out, extra_in, extra_out,
             swap_send, swap_recv, pass_send, pass_recv, part_send, part_recv, direct_send, direct_recv,
             relay_send, relay_recv, pair_send, pair_recv, tree_send, tree_recv, extra_recv):
    r = lax.axis_index("rows")
    s = lax.axis_index("samples")
    x = s // 2
    c = s % 2
    twin = s + 1 - 2 * c
    beside = (((x + 1) % 4) * 2 + c, ((x + 3) % 4) * 2 + c)
    odd = (r % 2) == 1
    even = jnp.logical_not(odd)
    level2 = (r % 4) == 2
    helper = (r % 8) == 0
    level4 = (r % 16) == 8
    root = (r % 16) == 0

    barrier = pltpu.get_barrier_semaphore()

    def greet(row, sample):
        pl.semaphore_signal(barrier, inc=1, device_id=(row, sample), device_id_type=MESH)

    def send(src, dst, sems, to):
        return pltpu.make_async_remote_copy(
            src_ref=src, dst_ref=dst, send_sem=sems[0], recv_sem=sems[1], device_id=to, device_id_type=MESH)

    greet(r, twin)
    greet(r, beside[0])
    greet(r, beside[1])

    @pl.when(odd)
    def _():
        greet(r - 1, s)

    @pl.when(even)
    def _():
        greet(jnp.where(helper, r + 2, jnp.where(level2, r - 1, r - 2)), s)
        greet(jnp.where(helper, r + 6, jnp.where(level2, r + 1, r + 2)), s)

    @pl.when(level4)
    def _():
        greet(r - 8, s)

    @pl.when(root)
    def _():
        greet(8, s)
        greet(24, s)

    pl.semaphore_wait(
        barrier, 4 + jnp.where(level2, 2, 0) + jnp.where(helper, 1, 0) + jnp.where(level4, 1, 0))

    def swap_copy(h):
        return send(
            pt_ref.at[pl.ds(pl.multiple_of(HALF * (1 - c), 8), HALF), pl.ds(512 * h, 512)], swap.at[h],
            (swap_send.at[h], swap_recv.at[h]), (r, twin))

    swap_copy(0).start()
    swap_copy(1).start()

    def share(d, first=0, count=SHARE):
        return pl.ds(pl.multiple_of(SHARE * ((x + d) % 4) + first, 8), count)

    def pass_copy(h, way):
        return send(
            half_sum.at[h, share(2, PART * way, PART), :], passing.at[h, way],
            (pass_send.at[h, way], pass_recv.at[h, way]), (r, beside[way]))

    def part_copy(h, way):
        return send(
            half_sum.at[h, share((1, 3)[way]), :], parts.at[h, way],
            (part_send.at[h, way], part_recv.at[h, way]), (r, beside[way]))

    for h in range(2):
        swap_copy(h).wait_recv()
        half_sum[h] = pt_ref[pl.ds(pl.multiple_of(HALF * c, 8), HALF), 512 * h:512 * h + 512] + swap[h]
        for way in range(2):
            pass_copy(h, way).start()
    for h in range(2):
        for way in range(2):
            pass_copy(h, way).wait_recv()
            mine = share((1, 3)[way], PART * way, PART)
            half_sum[h, mine, :] += passing[h, way]
            part_copy(h, way).start()

    def place(d, first=0, count=SHARE):
        return pl.ds(pl.multiple_of(HALF * c + SHARE * ((x + d) % 4) + first, 8), count)

    outs = (leaf_ref, stk_ref, up_ref)
    OFFSET = (1, 3)

    def direct_copy(n, way):
        src = (own.at[((x + OFFSET[way]) % 4) // 2], own_stk, climb_in)[n]
        return send(
            src, outs[n].at[place(0), :], (direct_send.at[n, way], direct_recv.at[n, way]), (r, beside[way]))

    def relay_copy(n, way):
        back = OFFSET[1 - way]
        region = outs[n].at[place(back, PART * way, PART), :]
        return send(region, region, (relay_send.at[n, way], relay_recv.at[n, way]), (r, beside[way]))

    first_of_pair = (x % 2) == 0
    mate = jnp.where(first_of_pair, beside[0], beside[1])

    def leaf_relay():
        region = leaf_ref.at[place(jnp.where(first_of_pair, 3, 1)), :]
        return send(region, region, (relay_send.at[0, 0], relay_recv.at[0, 0]), (r, mate))

    def pair_copy(n, d):
        region = outs[n].at[place(d), :]
        return send(region, region, (pair_send.at[n, d], pair_recv.at[n, d]), (r, twin))

    def spread(n):
        for way in range(2):
            direct_copy(n, way).start()
        pair_copy(n, 0).start()

    def collect(n):
        for way in range(2):
            direct_copy(n, way).wait_recv()
            if n > 0:
                relay_copy(n, way).start()
            pair_copy(n, OFFSET[1 - way]).start()
        if n == 0:
            leaf_relay().start()

    def finish(n):
        if n == 0:
            leaf_relay().wait_recv()
        else:
            for way in range(2):
                relay_copy(n, way).wait_recv()
        pair_copy(n, 2).start()

    for h in range(2):
        for way in range(2):
            part_copy(h, way).wait_recv()
        total = half_sum[h, share(0), :] + parts[h, 0] + parts[h, 1]
        own[h] = total
        own_stk[:, 256 * h:256 * h + 256] = pick(total, piv_ref[0, h:h + 1, :])
    stacked = own_stk[...]
    skeleton = pick(stacked, piv_ref[0, 2:3, :])

    def skeleton_copy():
        return send(below, climb_in.at[:, pl.ds(0, 256)], (tree_send.at[0], tree_recv.at[0]), (r + 1, s))

    @pl.when(odd)
    def _():
        climb_in[:, 256:] = skeleton

    @pl.when(even)
    def _():
        below[...] = skeleton
        skeleton_copy().start()

    leaf_ref[place(0), :] = own[x // 2]
    stk_ref[place(0), :] = stacked

    node_row = jnp.where(odd, 14 + r // 2, jnp.where(level2, 6 + r // 4, r // 16))
    side = jnp.where(odd, (r // 2) % 2, jnp.where(level2, (r // 4) % 2, r // 16))
    where_to = pl.ds(pl.multiple_of(256 * side, 128), 256)

    def tree_copy(to, sem):
        return send(climb_out, climb_in.at[:, where_to], (tree_send.at[sem], tree_recv.at[side]), (to, s))

    def aside_copy():
        return send(climb_out, extra_in.at[:, where_to], (tree_send.at[2], extra_recv.at[side]), (r - r % 8, s))

    def extra_copy():
        return send(extra_out, climb_in.at[:, pl.ds(0, 256)], (tree_send.at[3], tree_recv.at[0]), (r + 8, s))

    def arrived(buffer, sems, half):
        send(climb_out, buffer.at[:, pl.ds(256 * half, 256)], (tree_send.at[1], sems.at[half]), (r, twin)).wait_recv()

    def select():
        climb_out[...] = pick(climb_in[...], node_ref[pl.ds(node_row, 1), :])

    up_one = jnp.where(side == 0, r + 1, r - 1)
    up_two = jnp.where(side == 0, r + 2, r - 2)

    @pl.when(odd)
    def _():
        arrived(climb_in, tree_recv, 0)
        select()
        tree_copy(up_one, 1).start()

    spread(0)
    spread(1)

    @pl.when(level2)
    def _():
        arrived(climb_in, tree_recv, 0)
        arrived(climb_in, tree_recv, 1)
        select()
        aside_copy().start()
        tree_copy(up_two, 1).start()

    collect(0)
    collect(1)

    @pl.when(helper)
    def _():
        arrived(extra_in, extra_recv, 0)
        arrived(extra_in, extra_recv, 1)
        extra_out[...] = pick(extra_in[...], node_ref[pl.ds(2 + r // 8, 1), :])

    @pl.when(level4)
    def _():
        climb_in[:, 256:] = extra_out[...]
        arrived(climb_in, tree_recv, 0)
        select()
        tree_copy(16, 1).start()
        tree_copy(0, 2).start()

    @pl.when(root)
    def _():
        extra_copy().start()

    @pl.when(jnp.logical_or(root, (r % 8) == 4))
    def _():
        arrived(climb_in, tree_recv, 0)
        arrived(climb_in, tree_recv, 1)

    up_ref[place(0), :] = climb_in[...]
    spread(2)
    finish(0)
    finish(1)
    collect(2)
    finish(2)

    for h in range(2):
        swap_copy(h).wait_send()
        for way in range(2):
            pass_copy(h, way).wait_send()
            part_copy(h, way).wait_send()

    @pl.when(even)
    def _():
        skeleton_copy().wait_send()

    @pl.when(odd)
    def _():
        tree_copy(up_one, 1).wait_send()

    @pl.when(level2)
    def _():
        aside_copy().wait_send()
        tree_copy(up_two, 1).wait_send()

    @pl.when(root)
    def _():
        extra_copy().wait_send()

    @pl.when(level4)
    def _():
        tree_copy(16, 1).wait_send()
        tree_copy(0, 2).wait_send()

    leaf_relay().wait_send()
    for n in range(3):
        for way in range(2):
            direct_copy(n, way).wait_send()
            if n > 0:
                relay_copy(n, way).wait_send()
        for d in range(4):
            pair_copy(n, d).wait()


def gathered(partial_t, pivots, node_pivots):
    vmem = pl.BlockSpec(memory_space=pltpu.VMEM)
    f32 = jnp.float32
    dma = pltpu.SemaphoreType.DMA
    return pl.pallas_call(
        exchange,
        out_shape=[jax.ShapeDtypeStruct((384, 512), f32)] * 3,
        in_specs=[vmem] * 3, out_specs=[vmem] * 3,
        scratch_shapes=[
            pltpu.VMEM((2, HALF, 512), f32), pltpu.VMEM((2, HALF, 512), f32),
            pltpu.VMEM((2, 2, PART, 512), f32), pltpu.VMEM((2, 2, SHARE, 512), f32),
            pltpu.VMEM((2, SHARE, 512), f32), pltpu.VMEM((SHARE, 512), f32), pltpu.VMEM((SHARE, 256), f32),
            pltpu.VMEM((SHARE, 512), f32), pltpu.VMEM((SHARE, 256), f32),
            pltpu.VMEM((SHARE, 512), f32), pltpu.VMEM((SHARE, 256), f32),
            dma((2,)), dma((2,)), dma((2, 2)), dma((2, 2)), dma((2, 2)), dma((2, 2)), dma((3, 2)), dma((3, 2)),
            dma((3, 2)), dma((3, 2)), dma((3, 4)), dma((3, 4)), dma((4,)), dma((2,)), dma((2,)),
        ],
        compiler_params=pltpu.CompilerParams(collective_id=0, has_side_effects=True, vmem_limit_bytes=48 << 20),
        name="exchange",
    )(partial_t, pivots, node_pivots)


def on_device(matrix_block, sketch_matrix, local_pivots, upper_pivots):
    partial_t = lax.dot_general(
        sketch_matrix, matrix_block, (((0,), (1,)), ((), ())), preferred_element_type=jnp.float32)
    return tuple(bases(*gathered(partial_t, local_pivots, upper_pivots)))


def solution(mesh):
    in_specs = (P("rows", "samples"), P("samples", None), P("rows", None, None), P())
    out_specs = (P(("rows", "samples"), None), P("rows", None), P("rows", None))
    return jax.shard_map(
        on_device, mesh=mesh, in_specs=in_specs, out_specs=out_specs, check_vma=False
    )
```

time: 944 us -> 75.5 us (0.08); the launches traced: 929 us -> 75.4 us
  other arithmetic: 633 us -> 0 us
  matrix products: 129 us -> 4.73 us
  waiting for transfers between devices: 105 us -> 0 us
  Pallas kernels: 0 us -> 68.4 us
  local copies, waits for them, and re-layouts: 30.1 us -> 1.56 us
  between operations: 19.9 us -> 0.66 us
  starting transfers between devices: 12.5 us -> 0 us
    another operation x320 -> x0, other arithmetic: 614 us -> none  [the longest x192 331 us: inverse_factor(): lower_factor = jnp.linalg.cholesky(gram_matrix)]
    dot_general x241 -> x1, matrix products: 111 us -> 4.73 us  [on_device(): lax.dot_general(sketch_matrix, matrix_block, (((0,), (1,)), ((), ())), pr...]
    pallas_call x0 -> x2, Pallas kernels: none -> 68.4 us  [the longest x1 48.5 us: gathered(): pl.pallas_call(exchange, out_shape=[jax.ShapeDtypeStruct((384, 512), f32)...]
    psum x1 -> x0, waiting for transfers between devices: 66.2 us -> none  [on_device(): summed = lax.psum(partial_value, 'samples')]
    ppermute x5 -> x0, waiting for transfers between devices: 38.7 us -> none  [partner_2(): return lax.ppermute(block, axis, route)]
    another operation x64 -> x0, matrix products: 17.9 us -> none  [inverse_factor(): return jax.scipy.linalg.solve_triangular(lower_factor, identity, lower=True)]
    ppermute x5 -> x0, starting transfers between devices: 12.5 us -> none  [partner_2(): return lax.ppermute(block, axis, route)]
  transfers between devices with their start and end apart: 6 -> 0, of which waited for: 5 -> 0; matrix products, arithmetic and copies ran while one was open for 3% -> 0% of each run, Pallas kernels for 0% -> 0%
where the time goes in v3:
time: 75.5 us; the launch traced here: 75.4 us
  Pallas kernels  68.4 us (91%)
  matrix products  4.73 us (6%)
  local copies, waits for them, and re-layouts  1.56 us (2%)
    pallas_call x1, Pallas kernels, gathered(): pl.pallas_call(exchange, out_shape=[jax.ShapeDtypeStruct((384, 512), f32)...  48.5 us
    pallas_call x1, Pallas kernels, bases(): pl.pallas_call(factor, out_shape=[jax.ShapeDtypeStruct((128, 384), f32),...  19.9 us
    dot_general x1, matrix products, on_device(): lax.dot_general(sketch_matrix, matrix_block, (((0,), (1,)), ((), ())), pr...  4.73 us
    unnamed x5, local copies, waits for them, and re-layouts  1.56 us

profile of v3, /device:TPU:1, one launch (start us, length us, event | category | flops | bytes accessed | tf_op | source)
XLA Modules:
  0.0 75.4 jit_solution(9106673950024443581)
XLA Ops:
  0.6 0.0 copy-start
  0.6 0.8 %copy.7.piv_ref = s32[1,3,256]{2,1,0:T(4,128)S(1)} copy(s32[1,3,256]{2,0,1:T(1,128)} %param.6) | data formatting | bytes 6144 | tf_op args[2]
  1.5 0.7 copy-done
  2.2 0.0 copy-start.1
  2.2 4.7 %fusion.pt_ref = f32[384,1024]{1,0:T(8,128)S(1)} fusion(bf16[2560,384]{1,0:T(8,128)(2,1)S(1)} %copy-done, bf16[1024,2560]{1,0:T(8,128)(2,1)} %param.4), kind=kOutput, calls=%fused_computation | convolution fusion | flops 2013265920 | bytes 8781824 | tf_op jit(solution)/shard_map/dot_general | solution.py:441
  6.9 0.0 copy-done.1
  7.0 48.5 %exchange.1 = (f32[384,512]{1,0:T(8,128)S(1)}, f32[384,512]{1,0:T(8,128)S(1)}, f32[384,512]{1,0:T(8,128)S(1)}) custom-call(f32[384,1024]{1,0:T(8,128)S(1)} %fusion.pt_ref, s32[1,3,256]{2,1,0:T(4,128)S(1)} %copy.7.piv_ref, s32[30,256]{1,0:T(8,128)S(1)} %copy-done.1), custom_call_target="tpu_custom_call" | custom-call | tf_op jit(solution)/shard_map/exchange/pallas_call | solution.py:422
  55.5 19.9 %bases.1 = (f32[128,384]{1,0:T(8,128)}, f32[512,384]{1,0:T(8,128)}, f32[512,384]{1,0:T(8,128)}) custom-call(f32[384,512]{1,0:T(8,128)S(1)} %get-tuple-element.6.leaf_ref, f32[384,512]{1,0:T(8,128)S(1)} %get-tuple-element.7.stk_ref, f32[384,512]{1,0:T(8,128)S(1)} %get-tuple-element.8.up_ref), custom_call_target="tpu_custom_call" | custom-call | tf_op jit(solution)/shard_map/bases/pallas_call | solution.py:122
Async XLA Ops:
  0.6 1.6 %copy-start = (bf16[2560,384]{1,0:T(8,128)(2,1)S(1)}, bf16[2560,384]{1,0:T(8,128)(2,1)}, u32[]{:S(2)}) copy-start(bf16[2560,384]{1,0:T(8,128)(2,1)} %param.5) | copy-start | bytes 5898244
  2.2 4.7 %copy-start.1 = (s32[30,256]{1,0:T(8,128)S(1)}, s32[30,256]{1,0:T(8,128)}, u32[]{:S(2)}) copy-start(s32[30,256]{1,0:T(8,128)} %node_ref.1) | copy-start | bytes 92164

commit v4 on v3

--- a/solution.py
+++ b/solution.py
@@ -135,23 +135,30 @@
 PART = 24
 
 
-def pick(values, indices):
+def listed(indices, count):
+    rows = lax.broadcasted_iota(jnp.int32, (count, indices.shape[1]), 0)
+    return jnp.where(rows == indices, 1.0, 0.0).astype(jnp.bfloat16)
+
+
+def pick_by(values, chosen):
     high = values.astype(jnp.bfloat16)
     rest = values - high.astype(jnp.float32)
     middle = rest.astype(jnp.bfloat16)
     low = (rest - middle.astype(jnp.float32)).astype(jnp.bfloat16)
-    terms = jnp.concatenate([high, middle, low], 0)
-    rows = lax.broadcasted_iota(jnp.int32, (values.shape[1], indices.shape[1]), 0)
-    chosen = jnp.where(rows == indices, 1.0, 0.0).astype(jnp.bfloat16)
-    found = jnp.dot(terms, chosen, preferred_element_type=jnp.float32)
+    found = jnp.dot(jnp.concatenate([high, middle, low], 0), chosen, preferred_element_type=jnp.float32)
     count = values.shape[0]
     return found[:count] + found[count:2 * count] + found[2 * count:]
 
 
-def exchange(pt_ref, piv_ref, node_ref, leaf_ref, stk_ref, up_ref,
-             swap, half_sum, passing, parts, own, own_stk, below, climb_in, climb_out, extra_in, extra_out,
+def pick(values, indices):
+    return pick_by(values, listed(indices, values.shape[1]))
+
+
+def exchange(matrix_ref, sketch_ref, piv_ref, node_ref, leaf_ref, stk_ref, up_ref,
+             matrix, sketch, pt_ref, early, swap0, sum0, passing0, parts0, load,
+             swap, half_sum, passing, parts, own, own_stk, below, climb_in, climb_out, ring_in, composed, height3, column_in,
              swap_send, swap_recv, pass_send, pass_recv, part_send, part_recv, direct_send, direct_recv,
-             relay_send, relay_recv, pair_send, pair_recv, tree_send, tree_recv, extra_recv):
+             relay_send, relay_recv, pair_send, pair_recv, tree_send, tree_recv, ring_recv, column_recv):
     r = lax.axis_index("rows")
     s = lax.axis_index("samples")
     x = s // 2
@@ -165,6 +172,15 @@
     level4 = (r % 16) == 8
     root = (r % 16) == 0
 
+    def load_copy(i):
+        if i == 4:
+            return pltpu.make_async_copy(sketch_ref, sketch, load.at[4])
+        part = pl.ds(256 * i, 256)
+        return pltpu.make_async_copy(matrix_ref.at[part, :], matrix.at[part, :], load.at[i])
+
+    for i in (4, 0, 1, 2, 3):
+        load_copy(i).start()
+
     barrier = pltpu.get_barrier_semaphore()
 
     def greet(row, sample):
@@ -182,10 +198,15 @@
     def _():
         greet(r - 1, s)
 
-    @pl.when(even)
-    def _():
-        greet(jnp.where(helper, r + 2, jnp.where(level2, r - 1, r - 2)), s)
-        greet(jnp.where(helper, r + 6, jnp.where(level2, r + 1, r + 2)), s)
+    @pl.when(jnp.logical_and(even, jnp.logical_not(helper)))
+    def _():
+        greet(jnp.where(level2, r - 1, r - 2), s)
+        greet(jnp.where(level2, r + 1, r + 2), s)
+
+    @pl.when(helper)
+    def _():
+        for z in range(1, 8):
+            greet(r + z, s)
 
     @pl.when(level4)
     def _():
@@ -193,19 +214,49 @@
 
     @pl.when(root)
     def _():
-        greet(8, s)
-        greet(24, s)
-
-    pl.semaphore_wait(
-        barrier, 4 + jnp.where(level2, 2, 0) + jnp.where(helper, 1, 0) + jnp.where(level4, 1, 0))
+        for y in range(1, 4):
+            greet((r + 8 * y) % 32, s)
+
+    again = listed(piv_ref[0, 2:3, :], 512)
+    handed = [
+        jnp.dot(listed(piv_ref[0, h:h + 1, :], 512), again[256 * h:256 * h + 256],
+                preferred_element_type=jnp.float32).astype(jnp.bfloat16)
+        for h in range(2)
+    ]
+    load_copy(4).wait()
+    for i in range(4):
+        load_copy(i).wait()
+        product = jnp.dot(matrix[256 * i:256 * i + 256, :], sketch[...], preferred_element_type=jnp.float32)
+        pt_ref[:, 256 * i:256 * i + 256] = product.T
+    early[...] = pick_by(pt_ref[:, :512], handed[0]) + pick_by(pt_ref[:, 512:], handed[1])
+
+    pl.semaphore_wait(barrier, 5 + jnp.where(level2, 1, 0) + jnp.where(helper, 1, 0))
 
     def swap_copy(h):
         return send(
             pt_ref.at[pl.ds(pl.multiple_of(HALF * (1 - c), 8), HALF), pl.ds(512 * h, 512)], swap.at[h],
             (swap_send.at[h], swap_recv.at[h]), (r, twin))
 
+    def swap_early():
+        return send(
+            early.at[pl.ds(pl.multiple_of(HALF * (1 - c), 8), HALF), :], swap0,
+            (swap_send.at[2], swap_recv.at[2]), (r, twin))
+
+    swap_early().start()
     swap_copy(0).start()
     swap_copy(1).start()
+    group = r // 8
+
+    @pl.when(helper)
+    def _():
+        top = listed(node_ref[pl.ds(2 + group, 1), :], 512)
+        for q in range(2):
+            middle = jnp.dot(listed(node_ref[pl.ds(6 + 2 * group + q, 1), :], 512), top[256 * q:256 * q + 256],
+                             preferred_element_type=jnp.float32).astype(jnp.bfloat16)
+            for p in range(2):
+                lower = listed(node_ref[pl.ds(14 + 4 * group + 2 * q + p, 1), :], 512)
+                composed[512 * (2 * q + p):512 * (2 * q + p) + 512, :] = jnp.dot(
+                    lower, middle[256 * p:256 * p + 256], preferred_element_type=jnp.float32).astype(jnp.bfloat16)
 
     def share(d, first=0, count=SHARE):
         return pl.ds(pl.multiple_of(SHARE * ((x + d) % 4) + first, 8), count)
@@ -220,11 +271,62 @@
             half_sum.at[h, share((1, 3)[way]), :], parts.at[h, way],
             (part_send.at[h, way], part_recv.at[h, way]), (r, beside[way]))
 
-    for h in range(2):
+    def pass_early(way):
+        return send(
+            sum0.at[share(2, PART * way, PART), :], passing0.at[way],
+            (pass_send.at[2, way], pass_recv.at[2, way]), (r, beside[way]))
+
+    def part_early(way):
+        return send(
+            sum0.at[share((1, 3)[way]), :], parts0.at[way],
+            (part_send.at[2, way], part_recv.at[2, way]), (r, beside[way]))
+
+    swap_early().wait_recv()
+    sum0[...] = early[pl.ds(pl.multiple_of(HALF * c, 8), HALF), :] + swap0[...]
+    for way in range(2):
+        pass_early(way).start()
+    def pass_main(h):
         swap_copy(h).wait_recv()
         half_sum[h] = pt_ref[pl.ds(pl.multiple_of(HALF * c, 8), HALF), 512 * h:512 * h + 512] + swap[h]
         for way in range(2):
             pass_copy(h, way).start()
+
+    pass_main(0)
+    for way in range(2):
+        pass_early(way).wait_recv()
+        sum0[share((1, 3)[way], PART * way, PART), :] += passing0[way]
+        part_early(way).start()
+    pass_main(1)
+    for way in range(2):
+        part_early(way).wait_recv()
+    skeleton = sum0[share(0), :] + parts0[0] + parts0[1]
+
+    def skeleton_copy():
+        return send(below, climb_in.at[:, pl.ds(0, 256)], (tree_send.at[0], tree_recv.at[0]), (r + 1, s))
+
+    def ring_copy():
+        return send(
+            below, ring_in.at[:, pl.ds(pl.multiple_of(256 * (r % 8), 128), 256)],
+            (tree_send.at[2], ring_recv.at[r % 8]), (r - r % 8, s))
+
+    below[...] = skeleton
+
+    @pl.when(helper)
+    def _():
+        ring_in[:, :256] = skeleton
+
+    @pl.when(jnp.logical_not(helper))
+    def _():
+        ring_copy().start()
+
+    @pl.when(odd)
+    def _():
+        climb_in[:, 256:] = skeleton
+
+    @pl.when(even)
+    def _():
+        skeleton_copy().start()
+
     for h in range(2):
         for way in range(2):
             pass_copy(h, way).wait_recv()
@@ -238,10 +340,14 @@
     outs = (leaf_ref, stk_ref, up_ref)
     OFFSET = (1, 3)
 
-    def direct_copy(n, way):
-        src = (own.at[((x + OFFSET[way]) % 4) // 2], own_stk, climb_in)[n]
-        return send(
-            src, outs[n].at[place(0), :], (direct_send.at[n, way], direct_recv.at[n, way]), (r, beside[way]))
+    def direct_copy(n, way, part):
+        if n == 0:
+            src, dst = own.at[((x + OFFSET[way]) % 4) // 2], leaf_ref.at[place(0), :]
+        else:
+            first = PART * (way if part == 0 else 1 - way)
+            src = (own_stk, climb_in)[n - 1].at[pl.ds(first, PART), :]
+            dst = outs[n].at[place(0, first, PART), :]
+        return send(src, dst, (direct_send.at[n, way, part], direct_recv.at[n, way, part]), (r, beside[way]))
 
     def relay_copy(n, way):
         back = OFFSET[1 - way]
@@ -260,18 +366,22 @@
         return send(region, region, (pair_send.at[n, d], pair_recv.at[n, d]), (r, twin))
 
     def spread(n):
-        for way in range(2):
-            direct_copy(n, way).start()
+        for part in range(1 if n == 0 else 2):
+            for way in range(2):
+                direct_copy(n, way, part).start()
         pair_copy(n, 0).start()
 
     def collect(n):
         for way in range(2):
-            direct_copy(n, way).wait_recv()
+            direct_copy(n, way, 0).wait_recv()
             if n > 0:
                 relay_copy(n, way).start()
-            pair_copy(n, OFFSET[1 - way]).start()
         if n == 0:
             leaf_relay().start()
+        for way in range(2):
+            if n > 0:
+                direct_copy(n, way, 1).wait_recv()
+            pair_copy(n, OFFSET[1 - way]).start()
 
     def finish(n):
         if n == 0:
@@ -281,6 +391,41 @@
                 relay_copy(n, way).wait_recv()
         pair_copy(n, 2).start()
 
+    node_row = jnp.where(odd, 14 + r // 2, 6 + r // 4)
+    side = jnp.where(odd, (r // 2) % 2, (r // 4) % 2)
+    where_to = pl.ds(pl.multiple_of(256 * side, 128), 256)
+
+    def tree_copy(to, sem):
+        return send(climb_out, climb_in.at[:, where_to], (tree_send.at[sem], tree_recv.at[side]), (to, s))
+
+    mine_of_four = pl.ds(pl.multiple_of(256 * group, 128), 256)
+
+    def column_copy(which):
+        to = jnp.where(r == 0, 16, 0) if which == 0 else jnp.where(root, r + 8, 16)
+        return send(
+            height3, column_in.at[:, mine_of_four],
+            (tree_send.at[1 + 2 * which], column_recv.at[group]), (to, s))
+
+    def arrived(half):
+        send(climb_out, climb_in.at[:, pl.ds(256 * half, 256)],
+             (tree_send.at[1], tree_recv.at[half]), (r, twin)).wait_recv()
+
+    def column_arrived(y):
+        send(height3, column_in.at[:, pl.ds(pl.multiple_of(256 * y, 128), 256)],
+             (tree_send.at[1], column_recv.at[y]), (r, twin)).wait_recv()
+
+    def select():
+        climb_out[...] = pick(climb_in[...], node_ref[pl.ds(node_row, 1), :])
+
+    up_one = jnp.where(side == 0, r + 1, r - 1)
+    up_two = jnp.where(side == 0, r + 2, r - 2)
+
+    @pl.when(odd)
+    def _():
+        arrived(0)
+        select()
+        tree_copy(up_one, 1).start()
+
     for h in range(2):
         for way in range(2):
             part_copy(h, way).wait_recv()
@@ -288,95 +433,72 @@
         own[h] = total
         own_stk[:, 256 * h:256 * h + 256] = pick(total, piv_ref[0, h:h + 1, :])
     stacked = own_stk[...]
-    skeleton = pick(stacked, piv_ref[0, 2:3, :])
-
-    def skeleton_copy():
-        return send(below, climb_in.at[:, pl.ds(0, 256)], (tree_send.at[0], tree_recv.at[0]), (r + 1, s))
-
-    @pl.when(odd)
-    def _():
-        climb_in[:, 256:] = skeleton
-
-    @pl.when(even)
-    def _():
-        below[...] = skeleton
-        skeleton_copy().start()
-
     leaf_ref[place(0), :] = own[x // 2]
     stk_ref[place(0), :] = stacked
 
-    node_row = jnp.where(odd, 14 + r // 2, jnp.where(level2, 6 + r // 4, r // 16))
-    side = jnp.where(odd, (r // 2) % 2, jnp.where(level2, (r // 4) % 2, r // 16))
-    where_to = pl.ds(pl.multiple_of(256 * side, 128), 256)
-
-    def tree_copy(to, sem):
-        return send(climb_out, climb_in.at[:, where_to], (tree_send.at[sem], tree_recv.at[side]), (to, s))
-
-    def aside_copy():
-        return send(climb_out, extra_in.at[:, where_to], (tree_send.at[2], extra_recv.at[side]), (r - r % 8, s))
-
-    def extra_copy():
-        return send(extra_out, climb_in.at[:, pl.ds(0, 256)], (tree_send.at[3], tree_recv.at[0]), (r + 8, s))
-
-    def arrived(buffer, sems, half):
-        send(climb_out, buffer.at[:, pl.ds(256 * half, 256)], (tree_send.at[1], sems.at[half]), (r, twin)).wait_recv()
-
-    def select():
-        climb_out[...] = pick(climb_in[...], node_ref[pl.ds(node_row, 1), :])
-
-    up_one = jnp.where(side == 0, r + 1, r - 1)
-    up_two = jnp.where(side == 0, r + 2, r - 2)
-
-    @pl.when(odd)
-    def _():
-        arrived(climb_in, tree_recv, 0)
-        select()
-        tree_copy(up_one, 1).start()
-
     spread(0)
     spread(1)
 
     @pl.when(level2)
     def _():
-        arrived(climb_in, tree_recv, 0)
-        arrived(climb_in, tree_recv, 1)
+        arrived(0)
+        arrived(1)
         select()
-        aside_copy().start()
         tree_copy(up_two, 1).start()
+
+    @pl.when(helper)
+    def _():
+        for z in range(1, 8):
+            send(below, ring_in.at[:, pl.ds(256 * z, 256)],
+                 (tree_send.at[2], ring_recv.at[z]), (r, twin)).wait_recv()
+        found = pick_by(ring_in[...], composed[...])
+        height3[...] = found
+        column_in[:, mine_of_four] = found
+        for which in range(2):
+            column_copy(which).start()
 
     collect(0)
     collect(1)
 
-    @pl.when(helper)
-    def _():
-        arrived(extra_in, extra_recv, 0)
-        arrived(extra_in, extra_recv, 1)
-        extra_out[...] = pick(extra_in[...], node_ref[pl.ds(2 + r // 8, 1), :])
+    later = jnp.logical_or(odd, jnp.logical_or(level2, helper))
+
+    @pl.when(jnp.logical_not(later))
+    def _():
+        finish(0)
+        finish(1)
 
     @pl.when(level4)
     def _():
-        climb_in[:, 256:] = extra_out[...]
-        arrived(climb_in, tree_recv, 0)
-        select()
-        tree_copy(16, 1).start()
-        tree_copy(0, 2).start()
+        column_arrived(group - 1)
+        climb_in[...] = column_in[:, pl.ds(pl.multiple_of(512 * (group // 2), 128), 512)]
 
     @pl.when(root)
     def _():
-        extra_copy().start()
-
-    @pl.when(jnp.logical_or(root, (r % 8) == 4))
-    def _():
-        arrived(climb_in, tree_recv, 0)
-        arrived(climb_in, tree_recv, 1)
+        for y in range(1, 4):
+            column_arrived((group + y) % 4)
+        for j in range(2):
+            climb_in[:, 256 * j:256 * j + 256] = pick(column_in[:, 512 * j:512 * j + 512], node_ref[j:j + 1, :])
+
+    @pl.when((r % 8) == 4)
+    def _():
+        arrived(0)
+        arrived(1)
 
     up_ref[place(0), :] = climb_in[...]
     spread(2)
-    finish(0)
-    finish(1)
+
+    @pl.when(later)
+    def _():
+        finish(0)
+        finish(1)
+
     collect(2)
     finish(2)
 
+    swap_early().wait_send()
+    for way in range(2):
+        pass_early(way).wait_send()
+        part_early(way).wait_send()
     for h in range(2):
         swap_copy(h).wait_send()
         for way in range(2):
@@ -393,54 +515,56 @@
 
     @pl.when(level2)
     def _():
-        aside_copy().wait_send()
         tree_copy(up_two, 1).wait_send()
 
-    @pl.when(root)
-    def _():
-        extra_copy().wait_send()
-
-    @pl.when(level4)
-    def _():
-        tree_copy(16, 1).wait_send()
-        tree_copy(0, 2).wait_send()
+    @pl.when(helper)
+    def _():
+        for which in range(2):
+            column_copy(which).wait_send()
+
+    @pl.when(jnp.logical_not(helper))
+    def _():
+        ring_copy().wait_send()
 
     leaf_relay().wait_send()
     for n in range(3):
         for way in range(2):
-            direct_copy(n, way).wait_send()
+            direct_copy(n, way, 0).wait_send()
             if n > 0:
+                direct_copy(n, way, 1).wait_send()
                 relay_copy(n, way).wait_send()
         for d in range(4):
             pair_copy(n, d).wait()
 
 
-def gathered(partial_t, pivots, node_pivots):
+def gathered(matrix, sketch, pivots, node_pivots):
     vmem = pl.BlockSpec(memory_space=pltpu.VMEM)
     f32 = jnp.float32
     dma = pltpu.SemaphoreType.DMA
     return pl.pallas_call(
         exchange,
         out_shape=[jax.ShapeDtypeStruct((384, 512), f32)] * 3,
-        in_specs=[vmem] * 3, out_specs=[vmem] * 3,
+        in_specs=[pl.BlockSpec(memory_space=pltpu.MemorySpace.HBM)] * 2 + [vmem] * 2, out_specs=[vmem] * 3,
         scratch_shapes=[
+            pltpu.VMEM(matrix.shape, matrix.dtype), pltpu.VMEM(sketch.shape, sketch.dtype),
+            pltpu.VMEM((384, 1024), f32), pltpu.VMEM((384, 256), f32), pltpu.VMEM((HALF, 256), f32), pltpu.VMEM((HALF, 256), f32),
+            pltpu.VMEM((2, PART, 256), f32), pltpu.VMEM((2, SHARE, 256), f32), dma((5,)),
             pltpu.VMEM((2, HALF, 512), f32), pltpu.VMEM((2, HALF, 512), f32),
             pltpu.VMEM((2, 2, PART, 512), f32), pltpu.VMEM((2, 2, SHARE, 512), f32),
             pltpu.VMEM((2, SHARE, 512), f32), pltpu.VMEM((SHARE, 512), f32), pltpu.VMEM((SHARE, 256), f32),
             pltpu.VMEM((SHARE, 512), f32), pltpu.VMEM((SHARE, 256), f32),
-            pltpu.VMEM((SHARE, 512), f32), pltpu.VMEM((SHARE, 256), f32),
-            dma((2,)), dma((2,)), dma((2, 2)), dma((2, 2)), dma((2, 2)), dma((2, 2)), dma((3, 2)), dma((3, 2)),
-            dma((3, 2)), dma((3, 2)), dma((3, 4)), dma((3, 4)), dma((4,)), dma((2,)), dma((2,)),
+            pltpu.VMEM((SHARE, 2048), f32), pltpu.VMEM((2048, 256), jnp.bfloat16),
+            pltpu.VMEM((SHARE, 256), f32), pltpu.VMEM((SHARE, 1024), f32),
+            dma((3,)), dma((3,)), dma((3, 2)), dma((3, 2)), dma((3, 2)), dma((3, 2)), dma((3, 2, 2)), dma((3, 2, 2)),
+            dma((3, 2)), dma((3, 2)), dma((3, 4)), dma((3, 4)), dma((4,)), dma((2,)), dma((8,)), dma((4,)),
         ],
         compiler_params=pltpu.CompilerParams(collective_id=0, has_side_effects=True, vmem_limit_bytes=48 << 20),
         name="exchange",
-    )(partial_t, pivots, node_pivots)
+    )(matrix, sketch, pivots, node_pivots)
 
 
 def on_device(matrix_block, sketch_matrix, local_pivots, upper_pivots):
-    partial_t = lax.dot_general(
-        sketch_matrix, matrix_block, (((0,), (1,)), ((), ())), preferred_element_type=jnp.float32)
-    return tuple(bases(*gathered(partial_t, local_pivots, upper_pivots)))
+    return tuple(bases(*gathered(matrix_block, sketch_matrix, local_pivots, upper_pivots)))
 
 
 def solution(mesh):

time: 75.5 us -> 64.5 us (0.85)
  Pallas kernels: 68.4 us -> 60.7 us
  matrix products: 4.73 us -> 0 us
  local copies, waits for them, and re-layouts: 1.56 us -> 2.99 us
    pallas_call x1, Pallas kernels: 48.5 us -> 40.7 us  [gathered(): pl.pallas_call(exchange, out_shape=[jax.ShapeDtypeStruct((384, 512), f32)...]
    dot_general x1 -> x0, matrix products: 4.73 us -> none  [on_device(): lax.dot_general(sketch_matrix, matrix_block, (((0,), (1,)), ((), ())), pr...]
    unnamed x5, local copies, waits for them, and re-layouts: 1.56 us -> 2.99 us
where the time goes in v4:
time: 64.5 us; the launch traced here: 64.3 us
  Pallas kernels  60.7 us (94%)
  local copies, waits for them, and re-layouts  2.99 us (5%)
    pallas_call x1, Pallas kernels, gathered(): pl.pallas_call(exchange, out_shape=[jax.ShapeDtypeStruct((384, 512), f32)...  40.7 us
    pallas_call x1, Pallas kernels, bases(): pl.pallas_call(factor, out_shape=[jax.ShapeDtypeStruct((128, 384), f32),...  19.9 us
    unnamed x5, local copies, waits for them, and re-layouts  2.99 us

profile of v4, /device:TPU:1, one launch (start us, length us, event | category | flops | bytes accessed | tf_op | source)
XLA Modules:
  0.0 64.3 jit_solution(5578325632536486391)
XLA Ops:
  0.6 0.7 %copy.7.piv_ref = s32[1,3,256]{2,1,0:T(4,128)S(1)} copy(s32[1,3,256]{2,0,1:T(1,128)} %param.6) | data formatting | bytes 6144 | tf_op args[2]
  1.3 0.0 copy-start
  1.3 1.5 %copy-done = bf16[2560,384]{1,0:T(8,128)(2,1)S(1)} copy-done((bf16[2560,384]{1,0:T(8,128)(2,1)S(1)}, bf16[2560,384]{1,0:T(8,128)(2,1)}, u32[]{:S(2)}) %copy-start) | copy-done | bytes 1966104
  2.9 0.0 copy-start.1
  2.9 0.8 %copy-done.1 = s32[30,256]{1,0:T(8,128)S(1)} copy-done((s32[30,256]{1,0:T(8,128)S(1)}, s32[30,256]{1,0:T(8,128)}, u32[]{:S(2)}) %copy-start.1) | copy-done | bytes 30744
  3.6 40.7 %exchange.1 = (f32[384,512]{1,0:T(8,128)S(1)}, f32[384,512]{1,0:T(8,128)S(1)}, f32[384,512]{1,0:T(8,128)S(1)}) custom-call(bf16[1024,2560]{1,0:T(8,128)(2,1)} %matrix_ref.1, bf16[2560,384]{1,0:T(8,128)(2,1)S(1)} %copy-done, s32[1,3,256]{2,1,0:T(4,128)S(1)} %copy.7.piv_ref, s32[30,256]{1,0:T(8,128)S(1)} %copy-done.1), custom_call_target="tpu_custom_call" | custom-call | tf_op jit(solution)/shard_map/exchange/pallas_call | solution.py:544
  44.4 19.9 %bases.1 = (f32[128,384]{1,0:T(8,128)}, f32[512,384]{1,0:T(8,128)}, f32[512,384]{1,0:T(8,128)}) custom-call(f32[384,512]{1,0:T(8,128)S(1)} %get-tuple-element.6.leaf_ref, f32[384,512]{1,0:T(8,128)S(1)} %get-tuple-element.7.stk_ref, f32[384,512]{1,0:T(8,128)S(1)} %get-tuple-element.8.up_ref), custom_call_target="tpu_custom_call" | custom-call | tf_op jit(solution)/shard_map/bases/pallas_call | solution.py:122
Async XLA Ops:
  1.3 1.5 %copy-start = (bf16[2560,384]{1,0:T(8,128)(2,1)S(1)}, bf16[2560,384]{1,0:T(8,128)(2,1)}, u32[]{:S(2)}) copy-start(bf16[2560,384]{1,0:T(8,128)(2,1)} %sketch_ref.1) | copy-start | bytes 5898244
  2.9 0.8 %copy-start.1 = (s32[30,256]{1,0:T(8,128)S(1)}, s32[30,256]{1,0:T(8,128)}, u32[]{:S(2)}) copy-start(s32[30,256]{1,0:T(8,128)} %node_ref.1) | copy-start | bytes 92164

commit v5 on v4

--- a/solution.py
+++ b/solution.py
@@ -61,11 +61,12 @@
                 prow = lax.broadcasted_iota(jnp.int32, panel.shape, 0)
                 plane = lax.broadcasted_iota(jnp.int32, panel.shape, 1)
                 done = jnp.where((plane >= start) & (plane < rest) & (plane - start >= (prow // 8) * 8 + 8), 0.0, panel)
-                upd = mm(panel, done, TN)
+                upd = mm(panel.T[rest:], done, NN)
                 keep = m_ref[b, rest:, :]
                 lane2 = lax.broadcasted_iota(jnp.int32, keep.shape, 1)
                 keep = jnp.where((lane2 >= start) & (lane2 < rest), 0.0, keep)
-                m_ref[b, rest:, :] = keep - upd[rest:, :]
+                m_ref[b, rest:, :] = keep - upd
+
 
 def factor(leaf_ref, stk_ref, up_ref, leaf_o, stk_o, up_o, diag):
     srcs = (leaf_ref, stk_ref, up_ref)
@@ -558,7 +559,7 @@
             dma((3,)), dma((3,)), dma((3, 2)), dma((3, 2)), dma((3, 2)), dma((3, 2)), dma((3, 2, 2)), dma((3, 2, 2)),
             dma((3, 2)), dma((3, 2)), dma((3, 4)), dma((3, 4)), dma((4,)), dma((2,)), dma((8,)), dma((4,)),
         ],
-        compiler_params=pltpu.CompilerParams(collective_id=0, has_side_effects=True, vmem_limit_bytes=48 << 20),
+        compiler_params=pltpu.CompilerParams(collective_id=0, has_side_effects=True, vmem_limit_bytes=50 << 20),
         name="exchange",
     )(matrix, sketch, pivots, node_pivots)
 

time: 64.5 us -> 63 us (0.977)
  local copies, waits for them, and re-layouts: 2.99 us -> 1.44 us
    unnamed x5 -> x3, local copies, waits for them, and re-layouts: 2.99 us -> 1.44 us
where the time goes in v5:
time: 63 us; the launch traced here: 62.8 us
  Pallas kernels  60.8 us (97%)
  local copies, waits for them, and re-layouts  1.44 us (2%)
  between operations  0.64 us (1%)
    pallas_call x1, Pallas kernels, gathered(): pl.pallas_call(exchange, out_shape=[jax.ShapeDtypeStruct((384, 512), f32)...  41 us
    pallas_call x1, Pallas kernels, bases(): pl.pallas_call(factor, out_shape=[jax.ShapeDtypeStruct((128, 384), f32),...  19.7 us
    unnamed x3, local copies, waits for them, and re-layouts  1.44 us

profile of v5, /device:TPU:1, one launch (start us, length us, event | category | flops | bytes accessed | tf_op | source)
XLA Modules:
  0.0 62.8 jit_solution(1303222333968604229)
XLA Ops:
  0.6 0.7 %copy.7.piv_ref = s32[1,3,256]{2,1,0:T(4,128)S(1)} copy(s32[1,3,256]{2,0,1:T(1,128)} %param.6) | data formatting | bytes 6144 | tf_op args[2]
  1.3 0.0 copy-start
  1.3 0.8 %copy-done = s32[30,256]{1,0:T(8,128)S(1)} copy-done((s32[30,256]{1,0:T(8,128)S(1)}, s32[30,256]{1,0:T(8,128)}, u32[]{:S(2)}) %copy-start) | copy-done | bytes 30744
  2.1 41.0 %exchange.1 = (f32[384,512]{1,0:T(8,128)S(1)}, f32[384,512]{1,0:T(8,128)S(1)}, f32[384,512]{1,0:T(8,128)S(1)}) custom-call(bf16[1024,2560]{1,0:T(8,128)(2,1)} %matrix_ref.1, bf16[2560,384]{1,0:T(8,128)(2,1)} %sketch_ref.1, s32[1,3,256]{2,1,0:T(4,128)S(1)} %copy.7.piv_ref, s32[30,256]{1,0:T(8,128)S(1)} %copy-done), custom_call_target="tpu_custom_call" | custom-call | tf_op jit(solution)/shard_map/exchange/pallas_call | solution.py:545
  43.1 19.7 %bases.1 = (f32[128,384]{1,0:T(8,128)}, f32[512,384]{1,0:T(8,128)}, f32[512,384]{1,0:T(8,128)}) custom-call(f32[384,512]{1,0:T(8,128)S(1)} %get-tuple-element.6.leaf_ref, f32[384,512]{1,0:T(8,128)S(1)} %get-tuple-element.7.stk_ref, f32[384,512]{1,0:T(8,128)S(1)} %get-tuple-element.8.up_ref), custom_call_target="tpu_custom_call" | custom-call | tf_op jit(solution)/shard_map/bases/pallas_call | solution.py:123
Async XLA Ops:
  1.3 0.8 %copy-start = (s32[30,256]{1,0:T(8,128)S(1)}, s32[30,256]{1,0:T(8,128)}, u32[]{:S(2)}) copy-start(s32[30,256]{1,0:T(8,128)} %node_ref.1) | copy-start | bytes 92164

commit v6 on v5

--- a/solution.py
+++ b/solution.py
@@ -159,13 +159,14 @@
              matrix, sketch, pt_ref, early, swap0, sum0, passing0, parts0, load,
              swap, half_sum, passing, parts, own, own_stk, below, climb_in, climb_out, ring_in, composed, height3, column_in,
              swap_send, swap_recv, pass_send, pass_recv, part_send, part_recv, direct_send, direct_recv,
-             relay_send, relay_recv, pair_send, pair_recv, tree_send, tree_recv, ring_recv, column_recv):
+             relay_send, relay_recv, pair_send, pair_recv, tree_send, tree_recv, ring_recv, column_recv, cross_send, cross_recv):
     r = lax.axis_index("rows")
     s = lax.axis_index("samples")
     x = s // 2
     c = s % 2
     twin = s + 1 - 2 * c
     beside = (((x + 1) % 4) * 2 + c, ((x + 3) % 4) * 2 + c)
+    across = (((x + 1) % 4) * 2 + 1 - c, ((x + 3) % 4) * 2 + 1 - c)
     odd = (r % 2) == 1
     even = jnp.logical_not(odd)
     level2 = (r % 4) == 2
@@ -194,6 +195,8 @@
     greet(r, twin)
     greet(r, beside[0])
     greet(r, beside[1])
+    greet(r, across[0])
+    greet(r, across[1])
 
     @pl.when(odd)
     def _():
@@ -231,7 +234,7 @@
         pt_ref[:, 256 * i:256 * i + 256] = product.T
     early[...] = pick_by(pt_ref[:, :512], handed[0]) + pick_by(pt_ref[:, 512:], handed[1])
 
-    pl.semaphore_wait(barrier, 5 + jnp.where(level2, 1, 0) + jnp.where(helper, 1, 0))
+    pl.semaphore_wait(barrier, 7 + jnp.where(level2, 1, 0) + jnp.where(helper, 1, 0))
 
     def swap_copy(h):
         return send(
@@ -355,6 +358,14 @@
         region = outs[n].at[place(back, PART * way, PART), :]
         return send(region, region, (relay_send.at[n, way], relay_recv.at[n, way]), (r, beside[way]))
 
+    def cross_copy(way):
+        region = up_ref.at[place(OFFSET[1 - way], PART * way, PART), :]
+        return send(region, region, (cross_send.at[way], cross_recv.at[way]), (r, across[way]))
+
+    def cross_arrived(way):
+        region = up_ref.at[pl.ds(pl.multiple_of(HALF * (1 - c) + SHARE * ((x + 2) % 4) + PART * way, 8), PART), :]
+        send(region, region, (cross_send.at[way], cross_recv.at[way]), (r, across[way])).wait_recv()
+
     first_of_pair = (x % 2) == 0
     mate = jnp.where(first_of_pair, beside[0], beside[1])
 
@@ -377,6 +388,8 @@
             direct_copy(n, way, 0).wait_recv()
             if n > 0:
                 relay_copy(n, way).start()
+            if n == 2:
+                cross_copy(way).start()
         if n == 0:
             leaf_relay().start()
         for way in range(2):
@@ -390,7 +403,8 @@
         else:
             for way in range(2):
                 relay_copy(n, way).wait_recv()
-        pair_copy(n, 2).start()
+        if n < 2:
+            pair_copy(n, 2).start()
 
     node_row = jnp.where(odd, 14 + r // 2, 6 + r // 4)
     side = jnp.where(odd, (r // 2) % 2, (r // 4) % 2)
@@ -534,8 +548,11 @@
             if n > 0:
                 direct_copy(n, way, 1).wait_send()
                 relay_copy(n, way).wait_send()
-        for d in range(4):
+        for d in ((0, 1, 2, 3) if n < 2 else (0, 1, 3)):
             pair_copy(n, d).wait()
+    for way in range(2):
+        cross_copy(way).wait_send()
+        cross_arrived(way)
 
 
 def gathered(matrix, sketch, pivots, node_pivots):
@@ -557,7 +574,7 @@
             pltpu.VMEM((SHARE, 2048), f32), pltpu.VMEM((2048, 256), jnp.bfloat16),
             pltpu.VMEM((SHARE, 256), f32), pltpu.VMEM((SHARE, 1024), f32),
             dma((3,)), dma((3,)), dma((3, 2)), dma((3, 2)), dma((3, 2)), dma((3, 2)), dma((3, 2, 2)), dma((3, 2, 2)),
-            dma((3, 2)), dma((3, 2)), dma((3, 4)), dma((3, 4)), dma((4,)), dma((2,)), dma((8,)), dma((4,)),
+            dma((3, 2)), dma((3, 2)), dma((3, 4)), dma((3, 4)), dma((4,)), dma((2,)), dma((8,)), dma((4,)), dma((2,)), dma((2,)),
         ],
         compiler_params=pltpu.CompilerParams(collective_id=0, has_side_effects=True, vmem_limit_bytes=50 << 20),
         name="exchange",

time: 63 us -> 62.3 us (0.989)
  Pallas kernels: 60.8 us -> 60.1 us
    pallas_call x1, Pallas kernels: 41 us -> 40.3 us  [gathered(): pl.pallas_call(exchange, out_shape=[jax.ShapeDtypeStruct((384, 512), f32)...]
where the time goes in v6:
time: 62.3 us; the launch traced here: 62.1 us
  Pallas kernels  60.1 us (96%)
  local copies, waits for them, and re-layouts  1.44 us (2%)
  between operations  0.64 us (1%)
    pallas_call x1, Pallas kernels, gathered(): pl.pallas_call(exchange, out_shape=[jax.ShapeDtypeStruct((384, 512), f32)...  40.3 us
    pallas_call x1, Pallas kernels, bases(): pl.pallas_call(factor, out_shape=[jax.ShapeDtypeStruct((128, 384), f32),...  19.7 us
    unnamed x3, local copies, waits for them, and re-layouts  1.44 us

profile of v6, /device:TPU:1, one launch (start us, length us, event | category | flops | bytes accessed | tf_op | source)
XLA Modules:
  0.0 62.1 jit_solution(1900964643873995730)
XLA Ops:
  0.6 0.7 %copy.7.piv_ref = s32[1,3,256]{2,1,0:T(4,128)S(1)} copy(s32[1,3,256]{2,0,1:T(1,128)} %param.6) | data formatting | bytes 6144 | tf_op args[2]
  1.3 0.0 copy-start
  1.3 0.8 %copy-done = s32[30,256]{1,0:T(8,128)S(1)} copy-done((s32[30,256]{1,0:T(8,128)S(1)}, s32[30,256]{1,0:T(8,128)}, u32[]{:S(2)}) %copy-start) | copy-done | bytes 30744
  2.1 40.3 %exchange.1 = (f32[384,512]{1,0:T(8,128)S(1)}, f32[384,512]{1,0:T(8,128)S(1)}, f32[384,512]{1,0:T(8,128)S(1)}) custom-call(bf16[1024,2560]{1,0:T(8,128)(2,1)} %matrix_ref.1, bf16[2560,384]{1,0:T(8,128)(2,1)} %sketch_ref.1, s32[1,3,256]{2,1,0:T(4,128)S(1)} %copy.7.piv_ref, s32[30,256]{1,0:T(8,128)S(1)} %copy-done), custom_call_target="tpu_custom_call" | custom-call | tf_op jit(solution)/shard_map/exchange/pallas_call | solution.py:562
  42.4 19.7 %bases.1 = (f32[128,384]{1,0:T(8,128)}, f32[512,384]{1,0:T(8,128)}, f32[512,384]{1,0:T(8,128)}) custom-call(f32[384,512]{1,0:T(8,128)S(1)} %get-tuple-element.6.leaf_ref, f32[384,512]{1,0:T(8,128)S(1)} %get-tuple-element.7.stk_ref, f32[384,512]{1,0:T(8,128)S(1)} %get-tuple-element.8.up_ref), custom_call_target="tpu_custom_call" | custom-call | tf_op jit(solution)/shard_map/bases/pallas_call | solution.py:123
Async XLA Ops:
  1.3 0.8 %copy-start = (s32[30,256]{1,0:T(8,128)S(1)}, s32[30,256]{1,0:T(8,128)}, u32[]{:S(2)}) copy-start(s32[30,256]{1,0:T(8,128)} %node_ref.1) | copy-start | bytes 92164
